TPU v7x, 32 devices: a whole 2x2x4 slice. The times are simulated.
32 devices in a mesh: narrow: 4 (over z), wide: 8 (over y, x, core).
Axes of the slice: x: 2, y: 2, z: 4, core: 2. Of those that a mesh axis runs over, the one named last changes fastest.
Arguments:
- layer_input: bfloat16 [32, 512, 640], P(('narrow', 'wide')), may hold values from -6 to 6
- segments: int32 [32, 512], P(('narrow', 'wide')), may hold values from 0 to 7, never falling along the last dimension, each value on 1 to 192 neighbouring positions
- targets: int32 [32, 512], P(('narrow', 'wide')), may hold values from 0 to 24
- loss_mask: int32 [32, 512], P(('narrow', 'wide')), may hold values from 0 to 1
- readout: bfloat16 [640, 25], replicated, may hold values from -0.29882812 to 0.29882812
- attend_gain: bfloat16 [640], P('wide'), may hold values from 0.5 to 1.5
- attend_shift: bfloat16 [640], P('wide'), may hold values from -1.1953125 to 1.1953125
- heads_weight: bfloat16 [640, 1920], P('wide'), may hold values from -0.25 to 0.25
- query_bias: bfloat16 [640], P('wide'), may hold values from -1.1953125 to 1.1953125
- value_bias: bfloat16 [640], P('wide'), may hold values from -1.1953125 to 1.1953125
- output_weight: bfloat16 [640, 640], P('wide'), may hold values from -1.25 to 1.25
- output_bias: bfloat16 [640], P('wide'), may hold values from -1.1953125 to 1.1953125
- forward_gain: bfloat16 [640], P('wide'), may hold values from 0.5 to 1.5
- forward_shift: bfloat16 [640], P('wide'), may hold values from -1.1953125 to 1.1953125
- up_weight: bfloat16 [640, 5120], P('wide'), may hold values from -0.25 to 0.25
- up_bias: bfloat16 [5120], P('wide'), may hold values from -1.1953125 to 1.1953125
- down_weight: bfloat16 [5120, 640], P('wide'), may hold values from -0.125 to 0.125
- down_bias: bfloat16 [640], P('wide'), may hold values from -1.1953125 to 1.1953125
Outputs:
- layer_output: bfloat16 [32, 512, 640], P(('narrow', 'wide'))
- input_grad: float32 [32, 512, 640], P(('narrow', 'wide'))
- attend_gain_grad: float32 [640], P('wide')
- attend_shift_grad: float32 [640], P('wide')
- heads_weight_grad: float32 [640, 1920], P('wide')
- query_bias_grad: float32 [640], P('wide')
- value_bias_grad: float32 [640], P('wide')
- output_weight_grad: float32 [640, 640], P('wide')
- output_bias_grad: float32 [640], P('wide')
- forward_gain_grad: float32 [640], P('wide')
- forward_shift_grad: float32 [640], P('wide')
- up_weight_grad: float32 [640, 5120], P('wide')
- up_bias_grad: float32 [5120], P('wide')
- down_weight_grad: float32 [5120, 640], P('wide')
- down_bias_grad: float32 [640], P('wide')
- loss_sum: float32 [], replicated
- token_count: int32 [], replicated
All inputs are finite; a program needn't handle non-finite values.
Results may differ from a plain program's by a relative error of at most 0.013.
Values may be sent and summed in bfloat16 or wider, within the bound.
No kernel may reach another device: no remote copies, remote signals or barrier semaphores. Data moves between devices by JAX's collectives and lax.ppermute only.
A program may use at most 192 MiB of HBM per device.

v0:
```python
import math

import jax
import jax.numpy as jnp
from jax import lax
from jax.sharding import PartitionSpec as P

HEADS = 20
HEAD_DIM = 32


def normalize(values, gain, shift):
    average = jnp.mean(values, axis=-1, keepdims=True)
    centred = values - average
    spread = jnp.mean(centred * centred, axis=-1, keepdims=True)
    return centred * lax.rsqrt(spread + 1e-05) * gain + shift


def exact_gelu(values):
    return jax.nn.gelu(values, approximate=False)


def masked_scores(query_block, keyset, segment_block, segment_row):
    scale = 1.0 / math.sqrt(HEAD_DIM)
    scores = (
        jnp.einsum("qhd,khd->hqk", query_block, keyset, preferred_element_type=jnp.float32) * scale
    )
    allowed = (segment_block[:, None] == segment_row[None, :])[None]
    return jnp.where(allowed, scores, -1e30)


def local(
    layer_input,
    segments,
    targets,
    loss_mask,
    readout,
    attend_gain,
    attend_shift,
    heads_weight,
    query_bias,
    value_bias,
    output_weight,
    output_bias,
    forward_gain,
    forward_shift,
    up_weight,
    up_bias,
    down_weight,
    down_bias,
):
    length = layer_input.shape[1]
    width = layer_input.shape[2]
    block = min(512, length)
    count_blocks = length // block
    scale = 1.0 / math.sqrt(HEAD_DIM)
    inputs = layer_input[0].astype(jnp.float32)
    segment_row = segments[0]
    attend_set = (
        lax.all_gather(attend_gain, "wide", axis=0, tiled=True),
        lax.all_gather(attend_shift, "wide", axis=0, tiled=True),
        lax.all_gather(heads_weight, "wide", axis=0, tiled=True),
        lax.all_gather(query_bias, "wide", axis=0, tiled=True),
        lax.all_gather(value_bias, "wide", axis=0, tiled=True),
        lax.all_gather(output_weight, "wide", axis=0, tiled=True),
        lax.all_gather(output_bias, "wide", axis=0, tiled=True),
    )
    first_normed, first_pull = jax.vjp(
        normalize, inputs, attend_set[0].astype(jnp.float32), attend_set[1].astype(jnp.float32)
    )
    first_low = first_normed.astype(jnp.bfloat16)
    bias_row = jnp.concatenate(
        [attend_set[3], jnp.zeros_like(attend_set[3]), attend_set[4]]
    ).astype(jnp.float32)
    joined = (
        jnp.dot(first_low, attend_set[2], preferred_element_type=jnp.float32) + bias_row
    ).astype(jnp.bfloat16)
    split_heads = joined.reshape(length, 3, HEADS, HEAD_DIM)
    keyset = split_heads[:, 1]
    valueset = split_heads[:, 2]
    query_blocks = split_heads[:, 0].reshape(count_blocks, block, HEADS, HEAD_DIM)
    segment_blocks = segment_row.reshape(count_blocks, block)

    def forward_block(pieces):
        query_block, segment_block = pieces
        scores = masked_scores(query_block, keyset, segment_block, segment_row)
        highest = jnp.max(scores, axis=-1, keepdims=True)
        shifted = jnp.exp(scores - highest)
        totals = jnp.sum(shifted, axis=-1, keepdims=True)
        probs_low = (shifted / totals).astype(jnp.bfloat16)
        output = jnp.einsum("hqk,khd->qhd", probs_low, valueset, preferred_element_type=jnp.float32)
        return (output.astype(jnp.bfloat16), (highest + jnp.log(totals))[..., 0])

    attended_blocks, lse_blocks = lax.map(forward_block, (query_blocks, segment_blocks))
    attended = attended_blocks.reshape(length, width)
    middle = (
        inputs
        + jnp.dot(attended, attend_set[5], preferred_element_type=jnp.float32)
        + attend_set[6].astype(jnp.float32)
    )
    forward_set = (
        lax.all_gather(forward_gain, "wide", axis=0, tiled=True),
        lax.all_gather(forward_shift, "wide", axis=0, tiled=True),
        lax.all_gather(up_weight, "wide", axis=0, tiled=True),
        lax.all_gather(up_bias, "wide", axis=0, tiled=True),
        lax.all_gather(down_weight, "wide", axis=0, tiled=True),
        lax.all_gather(down_bias, "wide", axis=0, tiled=True),
    )
    second_normed, second_pull = jax.vjp(
        normalize, middle, forward_set[0].astype(jnp.float32), forward_set[1].astype(jnp.float32)
    )
    second_low = second_normed.astype(jnp.bfloat16)
    upward = jnp.dot(second_low, forward_set[2], preferred_element_type=jnp.float32) + forward_set[
        3
    ].astype(jnp.float32)
    activated, gelu_pull = jax.vjp(exact_gelu, upward)
    activated_low = activated.astype(jnp.bfloat16)
    result = (
        middle
        + jnp.dot(activated_low, forward_set[4], preferred_element_type=jnp.float32)
        + forward_set[5].astype(jnp.float32)
    )
    result_low = result.astype(jnp.bfloat16)
    logits = jnp.dot(result_low, readout, preferred_element_type=jnp.float32)
    highest_logit = jnp.max(logits, axis=-1, keepdims=True)
    shifted_logits = jnp.exp(logits - highest_logit)
    logit_totals = jnp.sum(shifted_logits, axis=-1, keepdims=True)
    log_total = highest_logit[:, 0] + jnp.log(logit_totals[:, 0])
    onehot = lax.broadcasted_iota(jnp.int32, logits.shape, 1) == targets[0][:, None]
    picked = jnp.sum(jnp.where(onehot, logits, 0.0), axis=-1)
    weights_row = loss_mask[0].astype(jnp.float32)
    loss_local = jnp.sum((log_total - picked) * weights_row)
    count_local = jnp.sum(weights_row)
    wide_count = lax.axis_size("wide")
    loss_column = jnp.full((wide_count,), loss_local)
    count_column = jnp.full((wide_count,), count_local)
    grad_logits = (
        weights_row[:, None] * (shifted_logits / logit_totals - onehot.astype(jnp.float32))
    ).astype(jnp.bfloat16)
    grad_result = jnp.einsum("lv,dv->ld", grad_logits, readout, preferred_element_type=jnp.float32)
    up_matrix, down_matrix = (
        lax.all_gather(up_weight, "wide", axis=0, tiled=True),
        lax.all_gather(down_weight, "wide", axis=0, tiled=True),
    )
    grad_down = grad_result.astype(jnp.bfloat16)
    down_weight_part = jnp.einsum(
        "lf,ld->fd", activated_low, grad_down, preferred_element_type=jnp.float32
    )
    down_bias_part = jnp.sum(grad_down, axis=0, dtype=jnp.float32)
    grad_activated = jnp.einsum(
        "ld,fd->lf", grad_down, down_matrix, preferred_element_type=jnp.float32
    )
    grad_up = gelu_pull(grad_activated)[0].astype(jnp.bfloat16)
    up_weight_part = jnp.einsum(
        "ld,lf->df", second_low, grad_up, preferred_element_type=jnp.float32
    )
    up_bias_part = jnp.sum(grad_up, axis=0, dtype=jnp.float32)
    grad_second = jnp.einsum("lf,df->ld", grad_up, up_matrix, preferred_element_type=jnp.float32)
    middle_part, forward_gain_part, forward_shift_part = second_pull(grad_second)
    grad_middle = grad_result + middle_part
    forward_shards = (
        lax.psum_scatter(forward_gain_part, "wide", scatter_dimension=0, tiled=True),
        lax.psum_scatter(forward_shift_part, "wide", scatter_dimension=0, tiled=True),
        lax.psum_scatter(up_weight_part, "wide", scatter_dimension=0, tiled=True),
        lax.psum_scatter(up_bias_part, "wide", scatter_dimension=0, tiled=True),
        lax.psum_scatter(down_weight_part, "wide", scatter_dimension=0, tiled=True),
        lax.psum_scatter(down_bias_part, "wide", scatter_dimension=0, tiled=True),
        lax.psum_scatter(loss_column, "wide", scatter_dimension=0, tiled=True),
        lax.psum_scatter(count_column, "wide", scatter_dimension=0, tiled=True),
    )
    heads_matrix, output_matrix = (
        lax.all_gather(heads_weight, "wide", axis=0, tiled=True),
        lax.all_gather(output_weight, "wide", axis=0, tiled=True),
    )
    grad_branch = grad_middle.astype(jnp.bfloat16)
    output_weight_part = jnp.einsum(
        "ld,le->de", attended, grad_branch, preferred_element_type=jnp.float32
    )
    output_bias_part = jnp.sum(grad_branch, axis=0, dtype=jnp.float32)
    grad_attended = jnp.einsum(
        "le,de->ld", grad_branch, output_matrix, preferred_element_type=jnp.float32
    ).astype(jnp.bfloat16)
    grad_blocks = grad_attended.reshape(count_blocks, block, HEADS, HEAD_DIM)

    def backward_block(carry, pieces):
        key_sum, value_sum = carry
        query_block, segment_block, grad_block, lse_block = pieces
        scores = masked_scores(query_block, keyset, segment_block, segment_row)
        probs = jnp.exp(scores - lse_block[..., None])
        value_sum = value_sum + jnp.einsum(
            "hqk,qhd->khd",
            probs.astype(jnp.bfloat16),
            grad_block,
            preferred_element_type=jnp.float32,
        )
        grad_probs = jnp.einsum(
            "qhd,khd->hqk", grad_block, valueset, preferred_element_type=jnp.float32
        )
        inner = jnp.sum(probs * grad_probs, axis=-1, keepdims=True)
        grad_scores = (probs * (grad_probs - inner)).astype(jnp.bfloat16)
        grad_query = (
            jnp.einsum("hqk,khd->qhd", grad_scores, keyset, preferred_element_type=jnp.float32)
            * scale
        )
        key_sum = (
            key_sum
            + jnp.einsum(
                "hqk,qhd->khd", grad_scores, query_block, preferred_element_type=jnp.float32
            )
            * scale
        )
        return ((key_sum, value_sum), grad_query)

    zero_heads = jnp.zeros((length, HEADS, HEAD_DIM), jnp.float32)
    (key_sum, value_sum), query_grads = lax.scan(
        backward_block,
        (zero_heads, zero_heads),
        (query_blocks, segment_blocks, grad_blocks, lse_blocks),
    )
    grad_joined = jnp.concatenate(
        [
            query_grads.reshape(length, width),
            key_sum.reshape(length, width),
            value_sum.reshape(length, width),
        ],
        axis=1,
    ).astype(jnp.bfloat16)
    heads_weight_part = jnp.einsum(
        "ld,le->de", first_low, grad_joined, preferred_element_type=jnp.float32
    )
    query_bias_part = jnp.sum(grad_joined[:, :width], axis=0, dtype=jnp.float32)
    value_bias_part = jnp.sum(grad_joined[:, 2 * width :], axis=0, dtype=jnp.float32)
    grad_first = jnp.einsum(
        "le,de->ld", grad_joined, heads_matrix, preferred_element_type=jnp.float32
    )
    input_part, attend_gain_part, attend_shift_part = first_pull(grad_first)
    input_grad = grad_middle + input_part
    attend_shards = (
        lax.psum_scatter(attend_gain_part, "wide", scatter_dimension=0, tiled=True),
        lax.psum_scatter(attend_shift_part, "wide", scatter_dimension=0, tiled=True),
        lax.psum_scatter(heads_weight_part, "wide", scatter_dimension=0, tiled=True),
        lax.psum_scatter(query_bias_part, "wide", scatter_dimension=0, tiled=True),
        lax.psum_scatter(value_bias_part, "wide", scatter_dimension=0, tiled=True),
        lax.psum_scatter(output_weight_part, "wide", scatter_dimension=0, tiled=True),
        lax.psum_scatter(output_bias_part, "wide", scatter_dimension=0, tiled=True),
    )
    summed = (
        lax.psum(attend_shards[0].astype(jnp.bfloat16), "narrow").astype(jnp.float32),
        lax.psum(attend_shards[1].astype(jnp.bfloat16), "narrow").astype(jnp.float32),
        lax.psum(attend_shards[2].astype(jnp.bfloat16), "narrow").astype(jnp.float32),
        lax.psum(attend_shards[3].astype(jnp.bfloat16), "narrow").astype(jnp.float32),
        lax.psum(attend_shards[4].astype(jnp.bfloat16), "narrow").astype(jnp.float32),
        lax.psum(attend_shards[5].astype(jnp.bfloat16), "narrow").astype(jnp.float32),
        lax.psum(attend_shards[6].astype(jnp.bfloat16), "narrow").astype(jnp.float32),
        lax.psum(forward_shards[0].astype(jnp.bfloat16), "narrow").astype(jnp.float32),
        lax.psum(forward_shards[1].astype(jnp.bfloat16), "narrow").astype(jnp.float32),
        lax.psum(forward_shards[2].astype(jnp.bfloat16), "narrow").astype(jnp.float32),
        lax.psum(forward_shards[3].astype(jnp.bfloat16), "narrow").astype(jnp.float32),
        lax.psum(forward_shards[4].astype(jnp.bfloat16), "narrow").astype(jnp.float32),
        lax.psum(forward_shards[5].astype(jnp.bfloat16), "narrow").astype(jnp.float32),
        lax.psum(forward_shards[6].astype(jnp.bfloat16), "narrow").astype(jnp.float32),
        lax.psum(forward_shards[7].astype(jnp.bfloat16), "narrow").astype(jnp.float32),
    )
    loss_total = summed[13][0]
    count_total = summed[14][0]
    return (
        result_low[None],
        input_grad[None],
        summed[0],
        summed[1],
        summed[2],
        summed[3],
        summed[4],
        summed[5],
        summed[6],
        summed[7],
        summed[8],
        summed[9],
        summed[10],
        summed[11],
        summed[12],
        loss_total,
        count_total.astype(jnp.int32),
    )


def solution(mesh):
    in_specs = (
        P(("narrow", "wide"), None, None),
        P(("narrow", "wide"), None),
        P(("narrow", "wide"), None),
        P(("narrow", "wide"), None),
        P(),
        P("wide"),
        P("wide"),
        P("wide", None),
        P("wide"),
        P("wide"),
        P("wide", None),
        P("wide"),
        P("wide"),
        P("wide"),
        P("wide", None),
        P("wide"),
        P("wide", None),
        P("wide"),
    )
    out_specs = (
        P(("narrow", "wide"), None, None),
        P(("narrow", "wide"), None, None),
        P("wide"),
        P("wide"),
        P("wide", None),
        P("wide"),
        P("wide"),
        P("wide", None),
        P("wide"),
        P("wide"),
        P("wide"),
        P("wide", None),
        P("wide"),
        P("wide", None),
        P("wide"),
        P(),
        P(),
    )
    return jax.shard_map(local, mesh=mesh, in_specs=in_specs, out_specs=out_specs, check_vma=False)
```

profile of v0, /device:TPU:0, one launch (start us, length us, event | category | flops | bytes accessed | tf_op | source)
XLA Modules:
  0.0 585.5 jit_solution(7206739429165697035)
XLA Ops:
  22.8 26.0 %all-reduce.20 = (bf16[640]{0:T(1024)(128)(2,1)S(1)}, bf16[640]{0:T(1024)(128)(2,1)S(1)}, bf16[640]{0:T(1024)(128)(2,1)S(1)}, bf16[640]{0:T(1024)(128)(2,1)S(1)}...) all-reduce(bf16[640]{0:T(1024)(128)(2,1)S(1)} %dynamic-update-slice, ...), channel_id=1, replica_groups=mesh['narrow'=4,'wide'=8] {'wide'}, use_global_device_ids=true, to_apply=%add.3 | all-reduce | flops 5120 | bytes 20480
  48.9 8.2 %all-gather = bf16[8,1,640]{2,1,0:T(2,128)(2,1)S(1)} all-gather(bf16[1,1,640]{2,1,0:T(2,128)(2,1)S(1)} %reshape.230), channel_id=1, replica_groups=mesh['narrow'=4,'wide'=8] {'wide'}, dimensions={0}, use_global_device_ids=true | all-gather | bytes 11520 | tf_op jit(solution)/shard_map/all_gather | solution.py:105
  58.1 12.8 %all_gather.48 = bf16[640,640]{1,0:T(8,128)(2,1)} all-gather(bf16[80,640]{1,0:T(8,128)(2,1)} %param.28), channel_id=1, replica_groups=mesh['narrow'=4,'wide'=8] {'wide'}, dimensions={0}, use_global_device_ids=true | all-gather | bytes 921600 | tf_op jit(solution)/shard_map/all_gather | solution.py:65
  71.0 5.1 add_convert_fusion.1
  76.1 2.8 copy.50
  78.9 3.6 fusion.64
  82.5 3.0 fusion
  85.5 4.1 copy-done.2
  89.7 3.9 fusion.28
  95.0 31.2 %multiply_convert_fusion.1 = (bf16[512,5120]{1,0:T(8,128)(2,1)}, f32[512,5120]{1,0:T(8,128)}, f32[512,5120]{1,0:T(8,128)}) fusion(f32[5120]{0:T(1024)S(1)} %bitcast.122, bf16[640,5120]{1,0:T(8,128)(2,1)} %all-gather.7.cloned.1.call-done, f32[512,640]{1,0:T(8,128)S(1)} %get-tuple-element.124, f32[640]{0:T(1024)S(1)} %convert_element_type.218, ...), kind=kOutput, calls=%fused_computation.14 | convolution fusion | flops 3530096640 | bytes 34108416 | tf_op jit(solution)/shard_map/dot_general | solution.py:113
  126.2 12.8 %all-gather.9.cloned.1.call-done = bf16[5120,640]{1,0:T(8,128)(2,1)} async-done(((bf16[640,640]{1,0:T(8,128)(2,1)}), bf16[5120,640]{1,0:T(8,128)(2,1)}) %all-gather.9.cloned.1.call-update) | async-done | bytes 6553616 | tf_op jit(solution)/shard_map/all_gather | solution.py:106
  139.0 8.7 %fusion.24 = bf16[512,640]{1,0:T(8,128)(2,1)S(1)} fusion(f32[512,640]{1,0:T(8,128)S(1)} %get-tuple-element.124, bf16[512,5120]{1,0:T(8,128)(2,1)} %get-tuple-element.115, bf16[5120,640]{1,0:T(8,128)(2,1)} %all-gather.9.cloned.1.call-done, f32[640]{0:T(1024)S(1)} %convert_element_type.222), kind=kOutput, calls=%fused_computation.50 | convolution fusion | flops 3356426240 | bytes 13765120 | tf_op jit(solution)/shard_map/dot_general | solution.py:120
  148.5 15.0 %convert_reduce_fusion = (f32[5120]{0:T(1024)S(1)}, bf16[512,5120]{1,0:T(8,128)(2,1)}) fusion(f32[512,5120]{1,0:T(8,128)} %get-tuple-element.116, bf16[5120,640]{1,0:T(8,128)(2,1)} %all-gather.9.cloned.1.call-done, f32[512,640]{1,0:T(8,128)S(1)} %fusion.39, f32[512,5120]{1,0:T(8,128)} %get-tuple-element.125, f32[5120]{0:T(1024)S(1)} %bitcast.123), kind=kOutput, calls=%fused_computation.11 | convolution fusion | flops 3400330240 | bytes 34119680 | tf_op jit(solution)/shard_map/ld,fd->lf/dot_general | solution.py:150
  163.5 8.5 %multiply_reduce_fusion.1 = (f32[640]{0:T(1024)S(1)}, f32[512]{0:T(512)S(1)}, f32[640]{0:T(1024)S(1)}, f32[512,640]{1,0:T(8,128)S(1)}) fusion(f32[512,640]{1,0:T(8,128)S(1)} %copy-done.4, f32[512]{0:T(512)S(1)} %fusion.45, f32[512]{0:T(512)S(1)} %broadcast_multiply_fusion, f32[640]{0:T(1024)S(1)} %convert_element_type.217, ...), kind=kOutput, calls=%fused_computation.60 | convolution fusion | flops 3358063104 | bytes 14431744 | tf_op jit(solution)/shard_map/lf,df->ld/dot_general | solution.py:158
  179.7 13.8 %multiply_reduce_fusion = (f32[20,512]{1,0:T(8,128)S(1)}, f32[20,512,512]{1,2,0:T(8,128)}) fusion(f32[20,512,512]{1,2,0:T(8,128)} %copy-done.2, f32[20,512]{1,0:T(8,128)S(1)} %log_add_fusion, bf16[512,20,32]{0,2,1:T(8,128)(2,1)} %bitcast.111, bf16[512,3,20,32]{0,3,2,1:T(8,128)(2,1)S(1)} %bitcast.108), kind=kOutput, calls=%fused_computation.1 | convolution fusion | flops 351262720 | bytes 43343872 | tf_op jit(solution)/shard_map/while/body/eval_jaxpr/qhd,khd->hqk/dot_general | solution.py:196
  193.5 14.9 %multiply_convert_fusion = bf16[20,512,512]{1,2,0:T(8,128)(2,1)S(1)} fusion(f32[20,512,512]{1,2,0:T(8,128)} %get-tuple-element.130, f32[20,512,512]{1,2,0:T(8,128)} %copy-done.2, f32[20,512]{1,0:T(8,128)S(1)} %get-tuple-element.129, f32[20,512]{1,0:T(8,128)S(1)} %log_add_fusion), kind=kLoop, calls=%fused_computation | loop fusion | flops 20971520 | bytes 52510720 | tf_op jit(solution)/shard_map/while/body/eval_jaxpr/convert_element_type | solution.py:200
  209.9 3.1 fusion.23
  213.1 9.1 %fusion.25 = bf16[20,32,512]{2,1,0:T(8,128)(2,1)S(1)} fusion(bf16[512,20,32]{0,2,1:T(8,128)(2,1)S(1)} %bitcast.112, f32[20,512,512]{1,2,0:T(8,128)} %copy-done.2, f32[20,512]{1,0:T(8,128)S(1)} %log_add_fusion), kind=kOutput, calls=%fused_computation.51 | convolution fusion | flops 346357760 | bytes 22323200 | tf_op jit(solution)/shard_map/while/body/eval_jaxpr/hqk,qhd->khd/dot_general | solution.py:190
  223.1 4.1 fusion.34
  228.6 12.2 %fusion.57 = f32[640,5120]{1,0:T(8,128)} fusion(bf16[512,5120]{1,0:T(8,128)(2,1)} %get-tuple-element.133, f32[512,640]{1,0:T(8,128)S(1)} %copy-done.5, f32[640]{0:T(1024)S(1)} %convert_element_type.218, f32[640]{0:T(1024)S(1)} %convert_element_type.217, f32[512]{0:T(512)S(1)} %fusion.45, f32[512]{0:T(512)S(1)} %broadcast_multiply_fusion), kind=kOutput, calls=%fused_computation.117 | convolution fusion | flops 3357081600 | bytes 19670016 | tf_op jit(solution)/shard_map/ld,lf->df/dot_general | solution.py:154
  240.9 12.1 %fusion.48 = f32[5120,640]{1,0:T(8,128)} fusion(bf16[512,5120]{1,0:T(8,128)(2,1)} %get-tuple-element.115, f32[512,640]{1,0:T(8,128)S(1)} %fusion.39), kind=kOutput, calls=%fused_computation.111 | convolution fusion | flops 3355770880 | bytes 19660800 | tf_op jit(solution)/shard_map/lf,ld->fd/dot_general | solution.py:146
  255.0 27.3 %reduce-scatter.5.cloned.1.call-done = f32[80,1920]{1,0:T(8,128)} async-done(((f32[640,1920]{1,0:T(8,128)}), f32[80,1920]{1,0:T(8,128)}) %reduce-scatter.5.cloned.1.call-update) | async-done | bytes 614416 | tf_op jit(solution)/shard_map/reduce_scatter | solution.py:241
  284.2 96.4 %reduce-scatter.9.cloned.1.call-done = f32[80,5120]{1,0:T(8,128)} async-done(((f32[640,5120]{1,0:T(8,128)}), f32[80,5120]{1,0:T(8,128)}) %reduce-scatter.9.cloned.1.call-update) | async-done | bytes 1638416 | tf_op jit(solution)/shard_map/reduce_scatter | solution.py:164
  380.5 2.4 convert_element_type.255
  382.9 95.9 %reduce-scatter.11.cloned.1.call-done = f32[640,640]{1,0:T(8,128)} async-done(((f32[5120,640]{1,0:T(8,128)}), f32[640,640]{1,0:T(8,128)}) %reduce-scatter.11.cloned.1.call-update) | async-done | bytes 1638416 | tf_op jit(solution)/shard_map/reduce_scatter | solution.py:166
  478.9 2.4 convert_element_type.260
  484.2 4.0 fusion.59
  492.0 25.0 %all-reduce.19 = (bf16[640]{0:T(1024)(128)(2,1)S(1)}, bf16[640]{0:T(1024)(128)(2,1)S(1)}, bf16[640]{0:T(1024)(128)(2,1)S(1)}, bf16[640]{0:T(1024)(128)(2,1)S(1)}...) all-reduce(f32[640]{0:T(1024)S(1)} %get-tuple-element.70, ...), channel_id=2, replica_groups=mesh['narrow'=4,'wide'=8] {'wide'}, use_global_device_ids=true, to_apply=%region_14.15.clone | all-reduce | flops 10256 | bytes 61536
  520.1 12.4 %all-reduce.21 = (bf16[80]{0:T(256)(128)(2,1)S(1)}, bf16[80]{0:T(256)(128)(2,1)S(1)}, bf16[80]{0:T(256)(128)(2,1)S(1)}, bf16[80]{0:T(256)(128)(2,1)S(1)}, bf16[8...) all-reduce(bf16[80]{0:T(256)(128)(2,1)S(1)} %dynamic-slice.47, ...), channel_id=1, replica_groups=mesh['narrow'=4,'wide'=8] {'narrow'}, use_global_device_ids=true, to_apply=%region_15.16 | all-reduce | flops 1282 | bytes 5128 | tf_op jit(solution)/shard_map/psum | solution.py:248
  538.6 29.3 %all-reduce.25.cloned.1.call-done = (bf16[80,1920]{1,0:T(8,128)(2,1)}, bf16[80,640]{1,0:T(8,128)(2,1)}, bf16[80,5120]{1,0:T(8,128)(2,1)}, bf16[640,640]{1,0:T(8,128)(2,1)}) async-done(((bf16[80,1920]{1,0:T(8,128)(2,1)}, bf16[80,640]{1,0:T(8,128)(2,1)}, bf16[80,5120]{1,0:T(8,128)(2,1)}, bf16[640,640]{1,0:T(8,128)(2,1)}), (bf16[80,1920]{1,0:T(8,128)(2,1)}, bf16[80,640]{1,0:T(8,128)(2,1)}, ...) | async-done | bytes 2048016 | tf_op jit(solution)/shard_map/psum | solution.py:250
  571.3 2.4 convert_element_type.256
  573.7 2.4 convert_element_type.261
  (166 shorter events, 49.7 us)
Async XLA Ops:
  7.2 140.5 %copy-start = (bf16[640,25]{0,1:T(8,128)(2,1)S(1)}, bf16[640,25]{0,1:T(8,128)(2,1)}, u32[]{:S(2)}) copy-start(bf16[640,25]{0,1:T(8,128)(2,1)} %param.22) | copy-start | bytes 96004
  7.2 63.8 %all-gather.5.cloned.1.call-start = ((), (), s32[]{:S(2)}) async-start(), calls=%async_computation.4 | async-start | bytes 2764800 | tf_op jit(solution)/shard_map/all_gather | solution.py:62
  7.9 87.0 %all-gather.7.cloned.1.call-start = ((), (), s32[]{:S(2)}) async-start(), calls=%async_computation.5 | async-start | bytes 7372800 | tf_op jit(solution)/shard_map/all_gather | solution.py:104
  8.7 130.3 %all-gather.9.cloned.1.call-start = ((), (), s32[]{:S(2)}) async-start(), calls=%async_computation.6 | async-start | bytes 7372800 | tf_op jit(solution)/shard_map/all_gather | solution.py:106
  9.4 243.9 %reduce-scatter.7.cloned.1.call-start = ((), (), s32[]{:S(2)}) async-start(), calls=%async_computation.8 | async-start | bytes 1843200 | tf_op jit(solution)/shard_map/reduce_scatter | solution.py:244
  11.4 64.7 %copy-start.23 = (f32[512]{0:T(512)}, f32[512]{0:T(512)S(1)}, u32[]{:S(2)}) copy-start(f32[512]{0:T(512)S(1)} %broadcast_multiply_fusion.1) | copy-start | bytes 6148
  13.4 62.7 %copy-start.27 = (f32[512]{0:T(512)}, f32[512]{0:T(512)S(1)}, u32[]{:S(2)}) copy-start(f32[512]{0:T(512)S(1)} %fusion.44) | copy-start | bytes 6148
  48.8 27.3 %copy-start.21 = (f32[640]{0:T(1024)}, f32[640]{0:T(1024)S(1)}, u32[]{:S(2)}) copy-start(f32[640]{0:T(1024)S(1)} %convert_element_type.208) | copy-start | bytes 7684
  48.8 27.2 %copy-start.31 = (f32[640]{0:T(1024)}, f32[640]{0:T(1024)S(1)}, u32[]{:S(2)}) copy-start(f32[640]{0:T(1024)S(1)} %convert_element_type.209) | copy-start | bytes 7684
  82.5 7.2 %copy-start.2 = (f32[20,512,512]{1,2,0:T(8,128)}, f32[20,512,512]{1,2,0:T(8,128)S(1)}, u32[]{:S(2)}) copy-start(f32[20,512,512]{1,2,0:T(8,128)S(1)} %get-tuple-element.122) | copy-start | bytes 62914564
  89.7 3.9 copy-start.8
  89.7 4.0 copy-start.15
  94.6 44.4 %copy-start.3 = (f32[512,640]{1,0:T(8,128)}, f32[512,640]{1,0:T(8,128)S(1)}, u32[]{:S(2)}) copy-start(f32[512,640]{1,0:T(8,128)S(1)} %get-tuple-element.124) | copy-start | bytes 3932164
  139.0 9.0 %copy-start.29 = (s32[1,512]{1,0:T(1,128)S(1)}, s32[1,512]{1,0:T(1,128)}, u32[]{:S(2)}) copy-start(s32[1,512]{1,0:T(1,128)} %param.20) | copy-start | bytes 6148
  148.5 15.0 %copy-start.4 = (f32[512,640]{1,0:T(8,128)S(1)}, f32[512,640]{1,0:T(8,128)}, u32[]{:S(2)}) copy-start(f32[512,640]{1,0:T(8,128)} %copy-done.3) | copy-start | bytes 3932164
  179.6 102.7 %reduce-scatter.5.cloned.1.call-start = ((), (), s32[]{:S(2)}) async-start(), calls=%async_computation.7 | async-start | bytes 5529600 | tf_op jit(solution)/shard_map/reduce_scatter | solution.py:241
  209.9 12.4 %copy-start.11 = (bf16[20,32,512]{2,1,0:T(8,128)(2,1)}, bf16[20,32,512]{2,1,0:T(8,128)(2,1)S(1)}, u32[]{:S(2)}) copy-start(bf16[20,32,512]{2,1,0:T(8,128)(2,1)S(1)} %fusion.22) | copy-start | bytes 1966084
  213.1 9.2 %copy-start.17 = (bf16[20,32,512]{2,1,0:T(8,128)(2,1)}, bf16[20,32,512]{2,1,0:T(8,128)(2,1)S(1)}, u32[]{:S(2)}) copy-start(bf16[20,32,512]{2,1,0:T(8,128)(2,1)S(1)} %fusion.23) | copy-start | bytes 1966084
  213.1 10.0 %copy-start.9 = (bf16[1,512,640]{2,1,0:T(8,128)(2,1)S(1)}, bf16[1,512,640]{2,1,0:T(8,128)(2,1)}, u32[]{:S(2)}) copy-start(bf16[1,512,640]{2,1,0:T(8,128)(2,1)} %param.18) | copy-start | bytes 1966084
  213.1 10.0 %copy-start.22 = (f32[640]{0:T(1024)S(1)}, f32[640]{0:T(1024)}, u32[]{:S(2)}) copy-start(f32[640]{0:T(1024)} %copy-done.21) | copy-start | bytes 7684
  213.1 10.0 %copy-start.24 = (f32[512]{0:T(512)S(1)}, f32[512]{0:T(512)}, u32[]{:S(2)}) copy-start(f32[512]{0:T(512)} %copy-done.23) | copy-start | bytes 6148
  213.1 10.0 %copy-start.28 = (f32[512]{0:T(512)S(1)}, f32[512]{0:T(512)}, u32[]{:S(2)}) copy-start(f32[512]{0:T(512)} %copy-done.27) | copy-start | bytes 6148
  213.1 10.0 %copy-start.32 = (f32[640]{0:T(1024)S(1)}, f32[640]{0:T(1024)}, u32[]{:S(2)}) copy-start(f32[640]{0:T(1024)} %copy-done.31) | copy-start | bytes 7684
  227.3 153.3 %reduce-scatter.9.cloned.1.call-start = ((), (), s32[]{:S(2)}) async-start(), calls=%async_computation.9 | async-start | bytes 14745600 | tf_op jit(solution)/shard_map/reduce_scatter | solution.py:164
  240.8 238.1 %reduce-scatter.11.cloned.1.call-start = ((), (), s32[]{:S(2)}) async-start(), calls=%async_computation.10 | async-start | bytes 14745600 | tf_op jit(solution)/shard_map/reduce_scatter | solution.py:166
  253.0 229.6 %copy-start.30 = (s32[1,512]{1,0:T(1,128)S(1)}, s32[1,512]{1,0:T(1,128)}, u32[]{:S(2)}) copy-start(s32[1,512]{1,0:T(1,128)} %param.21) | copy-start | bytes 6148
  253.0 230.8 %copy-start.12 = (bf16[20,32,512]{2,1,0:T(8,128)(2,1)S(1)}, bf16[20,32,512]{2,1,0:T(8,128)(2,1)}, u32[]{:S(2)}) copy-start(bf16[20,32,512]{2,1,0:T(8,128)(2,1)} %copy-done.11) | copy-start | bytes 1966084
  253.0 230.8 %copy-start.14 = (bf16[20,32,512]{2,1,0:T(8,128)(2,1)S(1)}, bf16[20,32,512]{2,1,0:T(8,128)(2,1)}, u32[]{:S(2)}) copy-start(bf16[20,32,512]{2,1,0:T(8,128)(2,1)} %copy-done.13) | copy-start | bytes 1966084
  253.0 314.8 %all-reduce.25.cloned.1.call-start = ((), (), s32[]{:S(2)}) async-start(), calls=%async_computation.11 | async-start | bytes 4096000 | tf_op jit(solution)/shard_map/psum | solution.py:250
  484.1 4.0 copy-start.26
  484.2 4.8 copy-start.7
  489.0 87.2 %copy-start.1 = (bf16[640,25]{0,1:T(8,128)(2,1)S(1)}, bf16[640,25]{0,1:T(8,128)(2,1)}, u32[]{:S(2)}) copy-start(bf16[640,25]{0,1:T(8,128)(2,1)} %param.22) | copy-start | bytes 96004
  (9 other events, 14.6 us)
Sparse Core Ops, SparseCore 0:
  9.9 32.1 all-gather.4
  44.0 46.4 all-gather.6
  92.4 46.5 all-gather.8
  179.7 38.6 reduce-scatter.6
  227.4 54.8 reduce-scatter.4
  285.8 94.7 reduce-scatter.8
  384.1 94.7 reduce-scatter.10
  482.7 85.1 all-reduce.24
where the time goes:
time: 589 us; the launch traced here: 586 us
  waiting for transfers between devices  264 us (45%)
  matrix products  141 us (24%)
  blocking collectives  84.5 us (14%)
  other arithmetic  48.6 us (8%)
  local copies, waits for them, and re-layouts  25.9 us (4%)
  between operations  20.5 us (3%)
    reduce_scatter x1, waiting for transfers between devices, local(): lax.psum_scatter(up_weight_part, 'wide', scatter_dimension=0, tiled=True)  96.4 us
    reduce_scatter x1, waiting for transfers between devices, local(): lax.psum_scatter(down_weight_part, 'wide', scatter_dimension=0, tiled=True)  95.9 us
    unnamed x2, blocking collectives  51 us
    dot_general x1, matrix products, local(): jnp.dot(second_low, forward_set[2], preferred_element_type=jnp.float32)  31.2 us
    psum x1, waiting for transfers between devices, local(): lax.psum(attend_shards[2].astype(jnp.bfloat16), 'narrow')  29.3 us
    reduce_scatter x1, waiting for transfers between devices, local(): lax.psum_scatter(heads_weight_part, 'wide', scatter_dimension=0, tiled=True)  27.3 us
    unnamed x96, local copies, waits for them, and re-layouts  19.7 us
    dot_general x1, matrix products, local(): jnp.einsum('ld,fd->lf', grad_down, down_matrix, preferred_element_type=jn...  15 us
  transfers between devices with their start and end apart: 8, of which 5 were waited for; matrix products, arithmetic and copies ran while one was open for 27% of the time, Pallas kernels for 0%

commit v1 on v0

v1 whole, which is shorter than its diff:
```python
import math

import jax
import jax.numpy as jnp
from jax import lax
from jax.sharding import PartitionSpec as P

HEADS = 20
HEAD_DIM = 32
LOSS_LANES = 128


def normalize(values, gain, shift):
    average = jnp.mean(values, axis=-1, keepdims=True)
    centred = values - average
    spread = jnp.mean(centred * centred, axis=-1, keepdims=True)
    return centred * lax.rsqrt(spread + 1e-05) * gain + shift


def exact_gelu(values):
    return jax.nn.gelu(values, approximate=False)


def swap(values, bit):
    return lax.ppermute(values, "wide", [(i, i ^ bit) for i in range(lax.axis_size("wide"))])


def same_core_groups():
    chips = lax.axis_size("wide") // 2
    return [[2 * chip + core for chip in range(chips)] for core in range(2)]


def spread_chips(shard):
    if lax.axis_size("wide") != 8:
        return lax.all_gather(shard, "wide", axis=0, axis_index_groups=same_core_groups())
    chip = lax.axis_index("wide") // 2
    half = shard.shape[0] // 2
    along_x = swap(shard, 2)
    along_y = swap(shard, 4)
    across = jnp.concatenate([swap(along_y[:half], 2), swap(along_x[half:], 4)])
    whole = jnp.zeros((4,) + shard.shape, shard.dtype)
    for offset, part in enumerate((shard, along_x, along_y, across)):
        whole = lax.dynamic_update_index_in_dim(whole, part, chip ^ offset, 0)
    return whole


def add_low(left, right):
    return (left.astype(jnp.float32) + right.astype(jnp.float32)).astype(jnp.bfloat16)


def collect_chips(parts):
    if lax.axis_size("wide") != 8:
        return lax.psum_scatter(
            parts, "wide", scatter_dimension=0, axis_index_groups=same_core_groups()
        )
    chip = lax.axis_index("wide") // 2
    half = parts.shape[1] // 2

    def pick(offset, low, high):
        return lax.dynamic_index_in_dim(parts, chip ^ offset, 0, keepdims=False)[low:high]

    size = parts.shape[1]
    from_x = swap(jnp.stack([pick(1, 0, half), pick(3, 0, half)]), 2)
    from_y = swap(jnp.stack([pick(2, half, size), pick(3, half, size)]), 4)
    upper_far = add_low(pick(2, 0, half), from_x[1])
    lower_far = add_low(pick(1, half, size), from_y[1])
    upper_got = swap(upper_far, 4)
    lower_got = swap(lower_far, 2)
    upper = add_low(add_low(pick(0, 0, half), from_x[0]), upper_got)
    lower = add_low(add_low(pick(0, half, size), from_y[0]), lower_got)
    return jnp.concatenate([upper, lower])


def sum_narrow(shard):
    if lax.axis_size("narrow") != 4:
        return lax.psum(shard, "narrow")
    place = lax.axis_index("narrow")
    inner = (place == 1) | (place == 2)
    half = add_low(shard, lax.ppermute(shard, "narrow", [(0, 1), (3, 2)]))
    total = add_low(half, lax.ppermute(half, "narrow", [(1, 2), (2, 1)]))
    outer = lax.ppermute(total, "narrow", [(1, 0), (2, 3)])
    return jnp.where(inner, total, outer)


def local(
    layer_input,
    segments,
    targets,
    loss_mask,
    readout,
    attend_gain,
    attend_shift,
    heads_weight,
    query_bias,
    value_bias,
    output_weight,
    output_bias,
    forward_gain,
    forward_shift,
    up_weight,
    up_bias,
    down_weight,
    down_bias,
):
    length = layer_input.shape[1]
    width = layer_input.shape[2]
    wide = lax.axis_size("wide")
    chips = wide // 2
    core = lax.axis_index("wide") % 2
    rows = heads_weight.shape[0]
    hidden = up_bias.shape[0]
    half = chips * hidden
    scale = 1.0 / math.sqrt(HEAD_DIM)
    inputs = layer_input[0].astype(jnp.float32)
    segment_row = segments[0]

    def by_core(mine, other, axis):
        return jnp.where(
            core == 0, jnp.stack([mine, other], axis), jnp.stack([other, mine], axis)
        )

    def mine_of(values, axis, flip=0):
        return lax.dynamic_index_in_dim(values, core ^ flip, axis, keepdims=False)

    attend_slab = jnp.concatenate([heads_weight, output_weight], axis=1)
    attend_mine = spread_chips(attend_slab)
    small = lax.all_gather(
        jnp.concatenate(
            [
                attend_gain,
                attend_shift,
                query_bias,
                value_bias,
                output_bias,
                forward_gain,
                forward_shift,
                down_bias,
                up_bias,
            ]
        ),
        "wide",
        axis=0,
    ).astype(jnp.float32)
    vectors = small[:, : 8 * rows].reshape(wide, 8, rows).transpose(1, 0, 2).reshape(8, width)
    up_bias_half = mine_of(small[:, 8 * rows :].reshape(chips, 2, hidden), 1).reshape(half)
    up_view = up_weight.reshape(rows, chips, 2, hidden)
    up_pair = by_core(mine_of(up_view, 2), swap(mine_of(up_view, 2, 1), 1), 0)
    up_half = spread_chips(up_pair.reshape(2 * rows, half)).reshape(width, half)
    down_half = spread_chips(down_weight).reshape(half, width)
    attend_full = by_core(attend_mine, swap(attend_mine, 1), 1).reshape(width, 4 * width)
    heads_full = attend_full[:, : 3 * width]
    output_full = attend_full[:, 3 * width :]

    first_normed, first_pull = jax.vjp(normalize, inputs, vectors[0], vectors[1])
    first_low = first_normed.astype(jnp.bfloat16)
    bias_row = jnp.concatenate([vectors[2], jnp.zeros_like(vectors[2]), vectors[3]])
    joined = (
        jnp.dot(first_low, heads_full, preferred_element_type=jnp.float32) + bias_row
    ).astype(jnp.bfloat16)
    split_heads = joined.reshape(length, 3, HEADS, HEAD_DIM)
    queryset = split_heads[:, 0]
    keyset = split_heads[:, 1]
    valueset = split_heads[:, 2]

    def masked_scores():
        scores = (
            jnp.einsum("qhd,khd->hqk", queryset, keyset, preferred_element_type=jnp.float32)
            * scale
        )
        allowed = (segment_row[:, None] == segment_row[None, :])[None]
        return jnp.where(allowed, scores, -1e30)

    scores = masked_scores()
    highest = jnp.max(scores, axis=-1, keepdims=True)
    shifted = jnp.exp(scores - highest)
    totals = jnp.sum(shifted, axis=-1, keepdims=True)
    probs_low = (shifted / totals).astype(jnp.bfloat16)
    attended = (
        jnp.einsum("hqk,khd->qhd", probs_low, valueset, preferred_element_type=jnp.float32)
        .astype(jnp.bfloat16)
        .reshape(length, width)
    )
    lse = highest + jnp.log(totals)
    middle = (
        inputs + jnp.dot(attended, output_full, preferred_element_type=jnp.float32) + vectors[4]
    )

    second_normed, second_pull = jax.vjp(normalize, middle, vectors[5], vectors[6])
    second_low = second_normed.astype(jnp.bfloat16)
    second_both = jnp.concatenate([second_low, swap(second_low, 1)])
    upward = jnp.dot(second_both, up_half, preferred_element_type=jnp.float32) + up_bias_half
    activated, gelu_pull = jax.vjp(exact_gelu, upward)
    activated_low = activated.astype(jnp.bfloat16)
    outward = jnp.dot(activated_low, down_half, preferred_element_type=jnp.float32)
    outward_got = swap(outward[length:].astype(jnp.bfloat16), 1)
    result = middle + (outward[:length] + outward_got.astype(jnp.float32)) + vectors[7]
    result_low = result.astype(jnp.bfloat16)

    logits = jnp.dot(result_low, readout, preferred_element_type=jnp.float32)
    highest_logit = jnp.max(logits, axis=-1, keepdims=True)
    shifted_logits = jnp.exp(logits - highest_logit)
    logit_totals = jnp.sum(shifted_logits, axis=-1, keepdims=True)
    log_total = highest_logit[:, 0] + jnp.log(logit_totals[:, 0])
    onehot = lax.broadcasted_iota(jnp.int32, logits.shape, 1) == targets[0][:, None]
    picked = jnp.sum(jnp.where(onehot, logits, 0.0), axis=-1)
    weights_row = loss_mask[0].astype(jnp.float32)
    loss_lanes = jnp.sum(((log_total - picked) * weights_row).reshape(-1, LOSS_LANES), axis=0)
    count_lanes = jnp.sum(weights_row.reshape(-1, LOSS_LANES), axis=0)
    grad_logits = (
        weights_row[:, None] * (shifted_logits / logit_totals - onehot.astype(jnp.float32))
    ).astype(jnp.bfloat16)
    grad_result = jnp.einsum("lv,dv->ld", grad_logits, readout, preferred_element_type=jnp.float32)

    grad_down = grad_result.astype(jnp.bfloat16)
    grad_down_both = jnp.concatenate([grad_down, swap(grad_down, 1)])
    down_weight_part = jnp.einsum(
        "lf,ld->fd", activated_low, grad_down_both, preferred_element_type=jnp.float32
    ).astype(jnp.bfloat16)
    down_weight_sum = collect_chips(down_weight_part.reshape(chips, hidden, width))
    down_weight_sum = sum_narrow(down_weight_sum)
    down_bias_part = jnp.sum(grad_down, axis=0, dtype=jnp.float32)
    grad_activated = jnp.einsum(
        "ld,fd->lf", grad_down_both, down_half, preferred_element_type=jnp.float32
    )
    grad_up = gelu_pull(grad_activated)[0].astype(jnp.bfloat16)
    up_weight_part = jnp.einsum(
        "ld,lf->df", second_both, grad_up, preferred_element_type=jnp.float32
    ).astype(jnp.bfloat16)
    up_weight_sum = collect_chips(up_weight_part.reshape(chips, 2 * rows, half))
    up_weight_sum = up_weight_sum.reshape(2, rows, half)
    up_weight_sum = by_core(
        mine_of(up_weight_sum, 0).reshape(rows, chips, hidden),
        swap(mine_of(up_weight_sum, 0, 1), 1).reshape(rows, chips, hidden),
        2,
    ).reshape(rows, 2 * half)
    up_weight_sum = sum_narrow(up_weight_sum)
    up_bias_part = jnp.sum(grad_up, axis=0, dtype=jnp.float32)
    inward = jnp.einsum("lf,df->ld", grad_up, up_half, preferred_element_type=jnp.float32)
    inward_got = swap(inward[length:].astype(jnp.bfloat16), 1)
    grad_second = inward[:length] + inward_got.astype(jnp.float32)
    middle_part, forward_gain_part, forward_shift_part = second_pull(grad_second)
    grad_middle = grad_result + middle_part

    grad_branch = grad_middle.astype(jnp.bfloat16)
    output_weight_part = jnp.einsum(
        "ld,le->de", attended, grad_branch, preferred_element_type=jnp.float32
    ).astype(jnp.bfloat16)
    output_bias_part = jnp.sum(grad_branch, axis=0, dtype=jnp.float32)
    grad_attended = (
        jnp.einsum("le,de->ld", grad_branch, output_full, preferred_element_type=jnp.float32)
        .astype(jnp.bfloat16)
        .reshape(length, HEADS, HEAD_DIM)
    )
    probs = jnp.exp(masked_scores() - lse)
    grad_value = jnp.einsum(
        "hqk,qhd->khd",
        probs.astype(jnp.bfloat16),
        grad_attended,
        preferred_element_type=jnp.float32,
    )
    grad_probs = jnp.einsum(
        "qhd,khd->hqk", grad_attended, valueset, preferred_element_type=jnp.float32
    )
    inner = jnp.sum(probs * grad_probs, axis=-1, keepdims=True)
    grad_scores = (probs * (grad_probs - inner)).astype(jnp.bfloat16)
    grad_query = (
        jnp.einsum("hqk,khd->qhd", grad_scores, keyset, preferred_element_type=jnp.float32)
        * scale
    )
    grad_key = (
        jnp.einsum("hqk,qhd->khd", grad_scores, queryset, preferred_element_type=jnp.float32)
        * scale
    )
    grad_joined = jnp.concatenate(
        [
            grad_query.reshape(length, width),
            grad_key.reshape(length, width),
            grad_value.reshape(length, width),
        ],
        axis=1,
    ).astype(jnp.bfloat16)
    heads_weight_part = jnp.einsum(
        "ld,le->de", first_low, grad_joined, preferred_element_type=jnp.float32
    ).astype(jnp.bfloat16)
    query_bias_part = jnp.sum(grad_joined[:, :width], axis=0, dtype=jnp.float32)
    value_bias_part = jnp.sum(grad_joined[:, 2 * width :], axis=0, dtype=jnp.float32)
    grad_first = jnp.einsum(
        "le,de->ld", grad_joined, heads_full, preferred_element_type=jnp.float32
    )
    input_part, attend_gain_part, attend_shift_part = first_pull(grad_first)
    input_grad = grad_middle + input_part

    short = jnp.stack(
        [
            attend_gain_part,
            attend_shift_part,
            query_bias_part,
            value_bias_part,
            output_bias_part,
            forward_gain_part,
            forward_shift_part,
            down_bias_part,
        ]
    )
    short = short.reshape(8, wide, rows).transpose(1, 0, 2).reshape(wide, 8 * rows)
    blank = jnp.zeros((chips, hidden), jnp.float32)
    up_bias_rows = by_core(up_bias_part.reshape(chips, hidden), blank, 1).reshape(wide, hidden)
    lanes = jnp.broadcast_to(
        jnp.concatenate([loss_lanes, count_lanes])[None], (wide, 2 * LOSS_LANES)
    )
    row = jnp.concatenate([short, up_bias_rows, lanes], axis=1).astype(jnp.bfloat16)
    used = row.shape[1]
    row = jnp.pad(row[:, None], ((0, 0), (0, 0), (0, 4 * width - used)))
    slab = jnp.concatenate(
        [
            jnp.concatenate(
                [
                    heads_weight_part.reshape(wide, rows, 3 * width),
                    output_weight_part.reshape(wide, rows, width),
                ],
                axis=2,
            ),
            row,
        ],
        axis=1,
    )
    slab = slab.reshape(chips, 2, rows + 1, 4 * width)
    slab = add_low(mine_of(slab, 1), swap(mine_of(slab, 1, 1), 1))
    slab = sum_narrow(collect_chips(slab)).astype(jnp.float32)
    last = slab[rows]
    vectors_sum = last[: 8 * rows].reshape(8, rows)
    lanes_sum = last[8 * rows + hidden : used].reshape(2, LOSS_LANES)
    return (
        result_low[None],
        input_grad[None],
        vectors_sum[0],
        vectors_sum[1],
        slab[:rows, : 3 * width],
        vectors_sum[2],
        vectors_sum[3],
        slab[:rows, 3 * width :],
        vectors_sum[4],
        vectors_sum[5],
        vectors_sum[6],
        up_weight_sum.astype(jnp.float32),
        last[8 * rows : 8 * rows + hidden],
        down_weight_sum.astype(jnp.float32),
        vectors_sum[7],
        jnp.sum(lanes_sum[0]),
        jnp.round(jnp.sum(lanes_sum[1])).astype(jnp.int32),
    )


def solution(mesh):
    in_specs = (
        P(("narrow", "wide"), None, None),
        P(("narrow", "wide"), None),
        P(("narrow", "wide"), None),
        P(("narrow", "wide"), None),
        P(),
        P("wide"),
        P("wide"),
        P("wide", None),
        P("wide"),
        P("wide"),
        P("wide", None),
        P("wide"),
        P("wide"),
        P("wide"),
        P("wide", None),
        P("wide"),
        P("wide", None),
        P("wide"),
    )
    out_specs = (
        P(("narrow", "wide"), None, None),
        P(("narrow", "wide"), None, None),
        P("wide"),
        P("wide"),
        P("wide", None),
        P("wide"),
        P("wide"),
        P("wide", None),
        P("wide"),
        P("wide"),
        P("wide"),
        P("wide", None),
        P("wide"),
        P("wide", None),
        P("wide"),
        P(),
        P(),
    )
    return jax.shard_map(local, mesh=mesh, in_specs=in_specs, out_specs=out_specs, check_vma=False)
```

time: 589 us -> 413 us (0.70)
  waiting for transfers between devices: 264 us -> 75 us
  blocking collectives: 84.5 us -> 24.6 us
  starting transfers between devices: 0.78 us -> 48 us
  local copies, waits for them, and re-layouts: 25.9 us -> 69.5 us
  matrix products: 141 us -> 112 us
  other arithmetic: 48.6 us -> 71.7 us
  between operations: 20.5 us -> 4.33 us
    reduce_scatter x4 -> x0, waiting for transfers between devices: 220 us -> none  [the longest x1 96.4 us: local(): lax.psum_scatter(up_weight_part, 'wide', scatter_dimension=0, tiled=True)]
    ppermute x0 -> x41, waiting for transfers between devices: none -> 75 us  [the longest x32 37.5 us: swap(): lax.ppermute(values, 'wide', [(i, i ^ bit) for i in range(lax.axis_size('...]
    unnamed x2 -> x0, blocking collectives: 51 us -> none
    ppermute x0 -> x41, starting transfers between devices: none -> 48 us  [the longest x32 26.4 us: swap(): lax.ppermute(values, 'wide', [(i, i ^ bit) for i in range(lax.axis_size('...]
    psum x1 -> x0, waiting for transfers between devices: 29.3 us -> none  [local(): lax.psum(attend_shards[2].astype(jnp.bfloat16), 'narrow')]
    dot_general x16, matrix products: 134 us -> 107 us  [the longest x1 28.2 us: local(): jnp.dot(second_both, up_half, preferred_element_type=jnp.float32)]
    slice x0 -> x17, local copies, waits for them, and re-layouts: none -> 13.4 us  [the longest x6 7.33 us: spread_chips(): across = jnp.concatenate([swap(along_y[:half], 2), swap(along_x[half:], 4)])]
    all_gather x3 -> x0, waiting for transfers between devices: 12.9 us -> none  [the longest x1 12.8 us: local(): lax.all_gather(down_weight, 'wide', axis=0, tiled=True)]
  transfers between devices with their start and end apart: 8 -> 41, of which waited for: 5 -> 16; matrix products, arithmetic and copies ran while one was open for 27% -> 46% of each run, Pallas kernels for 0% -> 0%
where the time goes in v1:
time: 413 us; the launch traced here: 405 us
  matrix products  112 us (27%)
  waiting for transfers between devices  75 us (18%)
  other arithmetic  71.7 us (17%)
  local copies, waits for them, and re-layouts  69.5 us (17%)
  starting transfers between devices  48 us (12%)
  blocking collectives  24.6 us (6%)
  between operations  4.33 us (1%)
    ppermute x32, waiting for transfers between devices, swap(): lax.ppermute(values, 'wide', [(i, i ^ bit) for i in range(lax.axis_size('...  37.5 us
    ppermute x3, waiting for transfers between devices, sum_narrow(): outer = lax.ppermute(total, 'narrow', [(1, 0), (2, 3)])  30.4 us
    dot_general x1, matrix products, local(): jnp.dot(second_both, up_half, preferred_element_type=jnp.float32)  28.2 us
    ppermute x32, starting transfers between devices, swap(): lax.ppermute(values, 'wide', [(i, i ^ bit) for i in range(lax.axis_size('...  26.4 us
    all_gather x1, blocking collectives, local(): lax.all_gather(jnp.concatenate([attend_gain, attend_shift, query_bias, va...  24.6 us
    unnamed x158, local copies, waits for them, and re-layouts  20.2 us
    ppermute x3, starting transfers between devices, sum_narrow(): half = add_low(shard, lax.ppermute(shard, 'narrow', [(0, 1), (3, 2)]))  15.4 us
    convert_element_type x1, other arithmetic, local(): grad_scores = (probs * (grad_probs - inner)).astype(jnp.bfloat16)  15 us
  transfers between devices with their start and end apart: 41, of which 16 were waited for; matrix products, arithmetic and copies ran while one was open for 46% of the time, Pallas kernels for 0%

profile of v1, /device:TPU:0, one launch (start us, length us, event | category | flops | bytes accessed | tf_op | source)
XLA Modules:
  0.0 404.8 jit_solution(1082702764833277928)
XLA Ops:
  15.3 24.6 %all-gather.1 = bf16[8,1,1280]{2,1,0:T(2,128)(2,1)S(1)} all-gather(bf16[1,1,1280]{2,1,0:T(2,128)(2,1)S(1)} %reshape.499), channel_id=2, replica_groups=mesh['narrow'=4,'wide'=8] {'wide'}, dimensions={0}, use_global_device_ids=true | all-gather | bytes 23040 | tf_op jit(solution)/shard_map/all_gather | solution.py:127
  70.2 8.9 %collective-permute-done.7 = bf16[160,2560]{1,0:T(8,128)(2,1)S(1)} collective-permute-done((bf16[160,2560]{1,0:T(8,128)(2,1)S(1)}, bf16[160,2560]{1,0:T(8,128)(2,1)S(1)}, u32[]{:S(2)}, u32[]{:S(2)}) %collective-permute-start.7) | collective-permute-done | bytes 819232 | tf_op jit(solution)/shard_map/ppermute | solution.py:25
  82.9 3.4 maximum_select_fusion
  88.0 3.3 add_convert_fusion.1
  94.0 3.6 fusion.100
  100.6 3.9 copy-done.2
  104.6 3.9 fusion.32
  116.2 28.2 %multiply_convert_fusion.1 = (bf16[1024,2560]{1,0:T(8,128)(2,1)S(1)}, f32[1024,2560]{1,0:T(8,128)}, f32[1024,2560]{1,0:T(8,128)}) fusion(f32[2560]{0:T(1024)S(1)} %add.293, bf16[640,2560]{1,0:T(8,128)(2,1)S(1)} %bitcast.241, bf16[512,640]{1,0:T(8,128)(2,1)S(1)} %collective-permute-done.5, bf16[512,640]{1,0:T(8,128)(2,1)S(1)} %add_convert_fusion.6), kind=kOutput, calls=%fused_computation.14 | convolution fusion | flops 3531079680 | bytes 30812160 | tf_op jit(solution)/shard_map/dot_general | solution.py:191
  144.4 4.2 %fusion.103 = f32[1024,640]{1,0:T(8,128)S(1)} fusion(bf16[1024,2560]{1,0:T(8,128)(2,1)S(1)} %get-tuple-element.44, bf16[2560,640]{1,0:T(8,128)(2,1)S(1)} %bitcast.243), kind=kOutput, calls=%fused_computation.274 | convolution fusion | flops 3355443200 | bytes 11141120 | tf_op jit(solution)/shard_map/dot_general | solution.py:194
  160.5 7.1 %convolution_convert_fusion = bf16[2560,640]{1,0:T(8,128)(2,1)S(1)} fusion(bf16[1024,2560]{1,0:T(8,128)(2,1)} %copy-done.71, bf16[512,640]{1,0:T(8,128)(2,1)} %collective-permute-done.16, bf16[512,640]{1,0:T(8,128)(2,1)} %get-tuple-element.39), kind=kOutput, calls=%fused_computation.31 | convolution fusion | flops 3359703040 | bytes 9830400 | tf_op jit(solution)/shard_map/lf,ld->fd/dot_general | solution.py:216
  171.8 13.5 %convert_reduce_fusion = (bf16[2560]{0:T(1024)(128)(2,1)S(1)}, bf16[1024,2560]{1,0:T(8,128)(2,1)}) fusion(f32[1024,2560]{1,0:T(8,128)} %get-tuple-element.45, bf16[2560,640]{1,0:T(8,128)(2,1)S(1)} %bitcast.244, bf16[512,640]{1,0:T(8,128)(2,1)} %collective-permute-done.16, bf16[512,640]{1,0:T(8,128)(2,1)} %get-tuple-element.39, ...), kind=kOutput, calls=%fused_computation.11 | convolution fusion | flops 3402626560 | bytes 30817280 | tf_op jit(solution)/shard_map/ld,fd->lf/dot_general | solution.py:222
  185.4 6.4 %fusion.104 = f32[1024,640]{1,0:T(8,128)S(1)} fusion(bf16[1024,2560]{1,0:T(8,128)(2,1)} %get-tuple-element.98, bf16[640,2560]{1,0:T(8,128)(2,1)S(1)} %bitcast.242), kind=kOutput, calls=%fused_computation.275 | convolution fusion | flops 3355443200 | bytes 11141120 | tf_op jit(solution)/shard_map/lf,df->ld/dot_general | solution.py:238
  194.2 3.9 convolution_convert_fusion.1
  211.1 13.0 %multiply_reduce_fusion = (f32[20,512]{1,0:T(8,128)S(1)}, f32[20,512,512]{1,2,0:T(8,128)}) fusion(f32[20,512,512]{1,2,0:T(8,128)} %copy-done.2, f32[20,512]{1,0:T(8,128)S(1)} %log_add_fusion, bf16[512,20,32]{0,2,1:T(8,128)(2,1)S(1)} %bitcast.233, bf16[512,3,20,32]{0,3,2,1:T(8,128)(2,1)S(1)} %bitcast.228), kind=kOutput, calls=%fused_computation.1 | convolution fusion | flops 351262720 | bytes 43343872 | tf_op jit(solution)/shard_map/qhd,khd->hqk/dot_general | solution.py:261
  224.1 15.0 %multiply_convert_fusion = bf16[20,512,512]{1,2,0:T(8,128)(2,1)S(1)} fusion(f32[20,512,512]{1,2,0:T(8,128)} %get-tuple-element.95, f32[20,512,512]{1,2,0:T(8,128)} %copy-done.2, f32[20,512]{1,0:T(8,128)S(1)} %get-tuple-element.94, f32[20,512]{1,0:T(8,128)S(1)} %log_add_fusion), kind=kLoop, calls=%fused_computation | loop fusion | flops 20971520 | bytes 52510720 | tf_op jit(solution)/shard_map/convert_element_type | solution.py:265
  240.8 3.1 fusion.28
  244.0 9.0 %bitcast_reduce_fusion = (bf16[20,32]{1,0:T(8,128)(2,1)S(1)}, bf16[20,32,512]{2,1,0:T(8,128)(2,1)S(1)}) fusion(bf16[512,20,32]{0,2,1:T(8,128)(2,1)S(1)} %bitcast.234, f32[20,512,512]{1,2,0:T(8,128)} %copy-done.2, f32[20,512]{1,0:T(8,128)S(1)} %log_add_fusion), kind=kOutput, calls=%fused_computation.133 | convolution fusion | flops 346684800 | bytes 22324480 | tf_op jit(solution)/shard_map/hqk,qhd->khd/dot_general | solution.py:255
  262.7 6.6 %reshape.482 = bf16[4,2,81,2560]{3,1,0,2:T(2,128)(2,1)S(1)} reshape(bf16[8,81,2560]{2,0,1:T(8,128)(2,1)} %fusion.13) | data formatting | bytes 6635520 | tf_op jit(solution)/shard_map/reshape | solution.py:327
  269.3 8.8 %constant_dynamic-slice_fusion.13 = (bf16[4,1,81,2560]{3,1,0,2:T(2,128)(2,1)}, f32[4,1,81,2560]{3,1,0,2:T(1,128)}) fusion(bf16[4,2,81,2560]{3,1,0,2:T(2,128)(2,1)S(1)} %reshape.482, s32[]{:T(128)S(6)} %select_n.180, s32[]{:T(128)S(6)} %select_n.179), kind=kLoop, calls=%fused_computation.219 | loop fusion | flops 829440 | bytes 8294408 | tf_op jit(solution)/shard_map/jit(dynamic_index_in_dim)/dynamic_slice | solution.py:123
  278.1 4.2 %copy.126 = bf16[4,1,81,2560]{3,0,1,2:T(4,128)(2,1)} copy(bf16[4,1,81,2560]{3,1,0,2:T(2,128)(2,1)} %get-tuple-element.46) | data formatting | bytes 3317760
  289.3 6.8 %collective-permute-done.35 = bf16[320,640]{1,0:T(8,128)(2,1)S(1)} collective-permute-done((bf16[320,640]{1,0:T(8,128)(2,1)S(1)}, bf16[320,640]{1,0:T(8,128)(2,1)S(1)}, u32[]{:S(2)}, u32[]{:S(2)}) %collective-permute-start.35) | collective-permute-done | bytes 409632 | tf_op jit(solution)/shard_map/ppermute | solution.py:25
  300.0 4.7 %collective-permute-start.38 = (bf16[640,640]{1,0:T(8,128)(2,1)}, bf16[640,640]{1,0:T(8,128)(2,1)}, u32[]{:S(2)}, u32[]{:S(2)}) collective-permute-start(bf16[640,640]{1,0:T(8,128)(2,1)} %pad_maximum_fusion.12), channel_id=1, source_target_pairs={{0,8},{24,16},{1,9},{25,17},{2,10},{26,18},{3,11},{27,19},{4,12},{... | collective-permute-start | bytes 2457608 | tf_op jit(solution)/shard_map/ppermute | solution.py:79
  311.4 3.2 select_n.192
  314.6 3.5 collective-permute-start.31
  318.2 3.6 collective-permute-done.38
  332.9 3.9 collective-permute-done.19
  344.5 4.9 %collective-permute-done.22 = bf16[41,2560]{1,0:T(8,128)(2,1)S(1)} collective-permute-done((bf16[41,2560]{1,0:T(8,128)(2,1)S(1)}, bf16[41,2560]{1,0:T(8,128)(2,1)S(1)}, u32[]{:S(2)}, u32[]{:S(2)}) %collective-permute-start.22) | collective-permute-done | bytes 209952 | tf_op jit(solution)/shard_map/ppermute | solution.py:25
  349.5 7.2 %collective-permute-start.23 = (bf16[81,2560]{1,0:T(8,128)(2,1)S(1)}, bf16[81,2560]{1,0:T(8,128)(2,1)S(1)}, u32[]{:S(2)}, u32[]{:S(2)}) collective-permute-start(bf16[81,2560]{1,0:T(8,128)(2,1)S(1)} %pad_maximum_fusion.15), channel_id=1, source_target_pairs={{0,8},{24,16},{1,9},{25,17},{2,10},{26,18},{3,11},{27,19},{4,12},{... | collective-permute-start | bytes 1244168 | tf_op jit(solution)/shard_map/ppermute | solution.py:79
  359.2 3.4 collective-permute-done.23
  364.9 15.4 %collective-permute-done.40 = bf16[640,640]{1,0:T(8,128)(2,1)S(1)} collective-permute-done((bf16[640,640]{1,0:T(8,128)(2,1)S(1)}, bf16[640,640]{1,0:T(8,128)(2,1)S(1)}, u32[]{:S(2)}, u32[]{:S(2)}) %collective-permute-start.40) | collective-permute-done | bytes 819232 | tf_op jit(solution)/shard_map/ppermute | solution.py:81
  383.0 11.5 %collective-permute-done.33 = bf16[80,5120]{1,0:T(8,128)(2,1)S(1)} collective-permute-done((bf16[80,5120]{1,0:T(8,128)(2,1)S(1)}, bf16[80,5120]{1,0:T(8,128)(2,1)S(1)}, u32[]{:S(2)}, u32[]{:S(2)}) %collective-permute-start.33) | collective-permute-done | bytes 819232 | tf_op jit(solution)/shard_map/ppermute | solution.py:81
  395.8 3.5 collective-permute-done.25
  (369 shorter events, 154.3 us)
Async XLA Ops:
  4.1 42.7 %collective-permute-start = (bf16[80,2560]{1,0:T(8,128)(2,1)}, bf16[80,2560]{1,0:T(8,128)(2,1)}, u32[]{:S(2)}, u32[]{:S(2)}) collective-permute-start(bf16[80,2560]{1,0:T(8,128)(2,1)} %constant_dynamic-update-slice_fusion), channel_id=1, source_target_pairs={{0,2},{1,3},{2,0},{3,1},{4,6},{5,7},{6,4},{7,5},{8,10},{9,11},{10,... | collective-permute-start | bytes 1228808 | tf_op jit(solution)/shard_map/ppermute | solution.py:25
  7.0 37.8 %collective-permute-start.1 = (bf16[80,2560]{1,0:T(8,128)(2,1)}, bf16[80,2560]{1,0:T(8,128)(2,1)}, u32[]{:S(2)}, u32[]{:S(2)}) collective-permute-start(bf16[80,2560]{1,0:T(8,128)(2,1)} %constant_dynamic-update-slice_fusion), channel_id=1, source_target_pairs={{0,4},{1,5},{2,6},{3,7},{4,0},{5,1},{6,2},{7,3},{8,12},{9,13},{10,... | collective-permute-start | bytes 1228808 | tf_op jit(solution)/shard_map/ppermute | solution.py:25
  8.6 55.1 %collective-permute-start.11 = (bf16[640,640]{1,0:T(8,128)(2,1)}, bf16[640,640]{1,0:T(8,128)(2,1)}, u32[]{:S(2)}, u32[]{:S(2)}) collective-permute-start(bf16[640,640]{1,0:T(8,128)(2,1)} %param.34), channel_id=1, source_target_pairs={{0,2},{1,3},{2,0},{3,1},{4,6},{5,7},{6,4},{7,5},{8,10},{9,11},{10,... | collective-permute-start | bytes 2457608 | tf_op jit(solution)/shard_map/ppermute | solution.py:25
  9.1 51.3 %collective-permute-start.12 = (bf16[640,640]{1,0:T(8,128)(2,1)}, bf16[640,640]{1,0:T(8,128)(2,1)}, u32[]{:S(2)}, u32[]{:S(2)}) collective-permute-start(bf16[640,640]{1,0:T(8,128)(2,1)} %param.34), channel_id=1, source_target_pairs={{0,4},{1,5},{2,6},{3,7},{4,0},{5,1},{6,2},{7,3},{8,12},{9,13},{10,... | collective-permute-start | bytes 2457608 | tf_op jit(solution)/shard_map/ppermute | solution.py:25
  15.2 39.8 %collective-permute-start.6 = (bf16[80,4,640]{2,0,1:T(8,128)(2,1)}, bf16[80,4,640]{2,0,1:T(8,128)(2,1)}, u32[]{:S(2)}, u32[]{:S(2)}) collective-permute-start(bf16[80,4,640]{2,0,1:T(8,128)(2,1)} %bitcast.221), channel_id=1, source_target_pairs={{0,1},{1,0},{2,3},{3,2},{4,5},{5,4},{6,7},{7,6},{8,9},{9,8},{10,11... | collective-permute-start | bytes 1228808 | tf_op jit(solution)/shard_map/ppermute | solution.py:25
  54.9 28.0 %collective-permute-start.4 = (bf16[4,80,2560]{2,1,0:T(8,128)(2,1)S(1)}, bf16[4,80,2560]{2,1,0:T(8,128)(2,1)}, u32[]{:S(2)}, u32[]{:S(2)}) collective-permute-start(bf16[4,80,2560]{2,1,0:T(8,128)(2,1)S(1)} %fusion.70), channel_id=1, source_target_pairs={{0,1},{1,0},{2,3},{3,2},{4,5},{5,4},{6,7},{7,6},{8,9},{9,8},{10,11... | collective-permute-start | bytes 4915208 | tf_op jit(solution)/shard_map/ppermute | solution.py:25
  57.9 21.2 %collective-permute-start.7 = (bf16[160,2560]{1,0:T(8,128)(2,1)S(1)}, bf16[160,2560]{1,0:T(8,128)(2,1)S(1)}, u32[]{:S(2)}, u32[]{:S(2)}) collective-permute-start(bf16[160,2560]{1,0:T(8,128)(2,1)S(1)} %bitcast.255), channel_id=1, source_target_pairs={{0,2},{1,3},{2,0},{3,1},{4,6},{5,7},{6,4},{7,5},{8,10},{9,11},{10,... | collective-permute-start | bytes 2457608 | tf_op jit(solution)/shard_map/ppermute | solution.py:25
  59.4 22.0 %collective-permute-start.8 = (bf16[160,2560]{1,0:T(8,128)(2,1)S(1)}, bf16[160,2560]{1,0:T(8,128)(2,1)S(1)}, u32[]{:S(2)}, u32[]{:S(2)}) collective-permute-start(bf16[160,2560]{1,0:T(8,128)(2,1)S(1)} %bitcast.256), channel_id=1, source_target_pairs={{0,4},{1,5},{2,6},{3,7},{4,0},{5,1},{6,2},{7,3},{8,12},{9,13},{10,... | collective-permute-start | bytes 2457608 | tf_op jit(solution)/shard_map/ppermute | solution.py:25
  62.2 49.5 %collective-permute-start.13 = (bf16[320,640]{1,0:T(8,128)(2,1)}, bf16[320,640]{1,0:T(8,128)(2,1)}, u32[]{:S(2)}, u32[]{:S(2)}) collective-permute-start(bf16[320,640]{1,0:T(8,128)(2,1)} %slice.382), channel_id=1, source_target_pairs={{0,2},{1,3},{2,0},{3,1},{4,6},{5,7},{6,4},{7,5},{8,10},{9,11},{10,... | collective-permute-start | bytes 1228808 | tf_op jit(solution)/shard_map/ppermute | solution.py:25
  65.5 46.2 %collective-permute-start.14 = (bf16[320,640]{1,0:T(8,128)(2,1)}, bf16[320,640]{1,0:T(8,128)(2,1)}, u32[]{:S(2)}, u32[]{:S(2)}) collective-permute-start(bf16[320,640]{1,0:T(8,128)(2,1)} %slice.383), channel_id=1, source_target_pairs={{0,4},{1,5},{2,6},{3,7},{4,0},{5,1},{6,2},{7,3},{8,12},{9,13},{10,... | collective-permute-start | bytes 1228808 | tf_op jit(solution)/shard_map/ppermute | solution.py:25
  79.9 34.5 %collective-permute-start.10 = (bf16[80,2560]{1,0:T(8,128)(2,1)}, bf16[80,2560]{1,0:T(8,128)(2,1)}, u32[]{:S(2)}, u32[]{:S(2)}) collective-permute-start(bf16[80,2560]{1,0:T(8,128)(2,1)} %slice.380), channel_id=1, source_target_pairs={{0,4},{1,5},{2,6},{3,7},{4,0},{5,1},{6,2},{7,3},{8,12},{9,13},{10,... | collective-permute-start | bytes 1228808 | tf_op jit(solution)/shard_map/ppermute | solution.py:25
  82.2 32.2 %collective-permute-start.9 = (bf16[80,2560]{1,0:T(8,128)(2,1)}, bf16[80,2560]{1,0:T(8,128)(2,1)}, u32[]{:S(2)}, u32[]{:S(2)}) collective-permute-start(bf16[80,2560]{1,0:T(8,128)(2,1)} %slice.379), channel_id=1, source_target_pairs={{0,2},{1,3},{2,0},{3,1},{4,6},{5,7},{6,4},{7,5},{8,10},{9,11},{10,... | collective-permute-start | bytes 1228808 | tf_op jit(solution)/shard_map/ppermute | solution.py:25
  168.8 113.5 %collective-permute-start.36 = (bf16[2,320,640]{2,1,0:T(8,128)(2,1)}, bf16[2,320,640]{2,1,0:T(8,128)(2,1)}, u32[]{:S(2)}, u32[]{:S(2)}) collective-permute-start(bf16[2,320,640]{2,1,0:T(8,128)(2,1)} %pad_maximum_fusion.11), channel_id=1, source_target_pairs={{0,4},{1,5},{2,6},{3,7},{4,0},{5,1},{6,2},{7,3},{8,12},{9,13},{10,... | collective-permute-start | bytes 2457608 | tf_op jit(solution)/shard_map/ppermute | solution.py:25
  171.2 111.1 %collective-permute-start.34 = (bf16[2,320,640]{2,1,0:T(8,128)(2,1)}, bf16[2,320,640]{2,1,0:T(8,128)(2,1)}, u32[]{:S(2)}, u32[]{:S(2)}) collective-permute-start(bf16[2,320,640]{2,1,0:T(8,128)(2,1)} %pad_maximum_fusion.10), channel_id=1, source_target_pairs={{0,2},{1,3},{2,0},{3,1},{4,6},{5,7},{6,4},{7,5},{8,10},{9,11},{10,... | collective-permute-start | bytes 2457608 | tf_op jit(solution)/shard_map/ppermute | solution.py:25
  194.1 8.4 %collective-permute-start.17 = (bf16[512,640]{1,0:T(8,128)(2,1)}, bf16[512,640]{1,0:T(8,128)(2,1)}, u32[]{:S(2)}, u32[]{:S(2)}) collective-permute-start(bf16[512,640]{1,0:T(8,128)(2,1)} %slice.500), channel_id=1, source_target_pairs={{0,1},{1,0},{2,3},{3,2},{4,5},{5,4},{6,7},{7,6},{8,9},{9,8},{10,11... | collective-permute-start | bytes 1966088 | tf_op jit(solution)/shard_map/ppermute | solution.py:25
  199.4 86.4 %collective-permute-start.28 = (bf16[2,80,2560]{2,1,0:T(8,128)(2,1)}, bf16[2,80,2560]{2,1,0:T(8,128)(2,1)}, u32[]{:S(2)}, u32[]{:S(2)}) collective-permute-start(bf16[2,80,2560]{2,1,0:T(8,128)(2,1)} %pad_maximum_fusion.8), channel_id=1, source_target_pairs={{0,4},{1,5},{2,6},{3,7},{4,0},{5,1},{6,2},{7,3},{8,12},{9,13},{10,... | collective-permute-start | bytes 2457608 | tf_op jit(solution)/shard_map/ppermute | solution.py:25
  201.9 83.8 %collective-permute-start.26 = (bf16[2,80,2560]{2,1,0:T(8,128)(2,1)}, bf16[2,80,2560]{2,1,0:T(8,128)(2,1)}, u32[]{:S(2)}, u32[]{:S(2)}) collective-permute-start(bf16[2,80,2560]{2,1,0:T(8,128)(2,1)} %pad_maximum_fusion.7), channel_id=1, source_target_pairs={{0,2},{1,3},{2,0},{3,1},{4,6},{5,7},{6,4},{7,5},{8,10},{9,11},{10,... | collective-permute-start | bytes 2457608 | tf_op jit(solution)/shard_map/ppermute | solution.py:25
  282.3 42.0 %collective-permute-start.18 = (bf16[4,81,2560]{2,0,1:T(4,128)(2,1)}, bf16[4,81,2560]{2,0,1:T(4,128)(2,1)}, u32[]{:S(2)}, u32[]{:S(2)}) collective-permute-start(bf16[4,81,2560]{2,0,1:T(4,128)(2,1)} %bitcast.220), channel_id=1, source_target_pairs={{0,1},{1,0},{2,3},{3,2},{4,5},{5,4},{6,7},{7,6},{8,9},{9,8},{10,11... | collective-permute-start | bytes 4976648 | tf_op jit(solution)/shard_map/ppermute | solution.py:25
  283.7 12.4 %collective-permute-start.35 = (bf16[320,640]{1,0:T(8,128)(2,1)S(1)}, bf16[320,640]{1,0:T(8,128)(2,1)S(1)}, u32[]{:S(2)}, u32[]{:S(2)}) collective-permute-start(bf16[320,640]{1,0:T(8,128)(2,1)S(1)} %get-tuple-element.50), channel_id=1, source_target_pairs={{0,4},{1,5},{2,6},{3,7},{4,0},{5,1},{6,2},{7,3},{8,12},{9,13},{10,... | collective-permute-start | bytes 1228808 | tf_op jit(solution)/shard_map/ppermute | solution.py:25
  285.1 12.3 %collective-permute-start.37 = (bf16[320,640]{1,0:T(8,128)(2,1)S(1)}, bf16[320,640]{1,0:T(8,128)(2,1)S(1)}, u32[]{:S(2)}, u32[]{:S(2)}) collective-permute-start(bf16[320,640]{1,0:T(8,128)(2,1)S(1)} %get-tuple-element.51), channel_id=1, source_target_pairs={{0,2},{1,3},{2,0},{3,1},{4,6},{5,7},{6,4},{7,5},{8,10},{9,11},{10,... | collective-permute-start | bytes 1228808 | tf_op jit(solution)/shard_map/ppermute | solution.py:25
  287.2 17.6 %collective-permute-start.27 = (bf16[80,2560]{1,0:T(8,128)(2,1)S(1)}, bf16[80,2560]{1,0:T(8,128)(2,1)S(1)}, u32[]{:S(2)}, u32[]{:S(2)}) collective-permute-start(bf16[80,2560]{1,0:T(8,128)(2,1)S(1)} %get-tuple-element.58), channel_id=1, source_target_pairs={{0,4},{1,5},{2,6},{3,7},{4,0},{5,1},{6,2},{7,3},{8,12},{9,13},{10,... | collective-permute-start | bytes 1228808 | tf_op jit(solution)/shard_map/ppermute | solution.py:25
  288.8 16.7 %collective-permute-start.29 = (bf16[80,2560]{1,0:T(8,128)(2,1)S(1)}, bf16[80,2560]{1,0:T(8,128)(2,1)S(1)}, u32[]{:S(2)}, u32[]{:S(2)}) collective-permute-start(bf16[80,2560]{1,0:T(8,128)(2,1)S(1)} %get-tuple-element.59), channel_id=1, source_target_pairs={{0,2},{1,3},{2,0},{3,1},{4,6},{5,7},{6,4},{7,5},{8,10},{9,11},{10,... | collective-permute-start | bytes 1228808 | tf_op jit(solution)/shard_map/ppermute | solution.py:25
  300.0 21.7 %collective-permute-start.38 = (bf16[640,640]{1,0:T(8,128)(2,1)}, bf16[640,640]{1,0:T(8,128)(2,1)}, u32[]{:S(2)}, u32[]{:S(2)}) collective-permute-start(bf16[640,640]{1,0:T(8,128)(2,1)} %pad_maximum_fusion.12), channel_id=1, source_target_pairs={{0,8},{24,16},{1,9},{25,17},{2,10},{26,18},{3,11},{27,19},{4,12},{... | collective-permute-start | bytes 2457608 | tf_op jit(solution)/shard_map/ppermute | solution.py:79
  314.6 42.1 %collective-permute-start.31 = (bf16[80,5120]{1,0:T(8,128)(2,1)}, bf16[80,5120]{1,0:T(8,128)(2,1)S(1)}, u32[]{:S(2)}, u32[]{:S(2)}) collective-permute-start(bf16[80,5120]{1,0:T(8,128)(2,1)} %select_n.192), channel_id=1, source_target_pairs={{0,8},{24,16},{1,9},{25,17},{2,10},{26,18},{3,11},{27,19},{4,12},{... | collective-permute-start | bytes 2457608 | tf_op jit(solution)/shard_map/ppermute | solution.py:79
  323.3 34.3 %collective-permute-start.39 = (bf16[640,640]{1,0:T(8,128)(2,1)S(1)}, bf16[640,640]{1,0:T(8,128)(2,1)S(1)}, u32[]{:S(2)}, u32[]{:S(2)}) collective-permute-start(bf16[640,640]{1,0:T(8,128)(2,1)S(1)} %add_convert_fusion.3), channel_id=1, source_target_pairs={{8,16},{16,8},{9,17},{17,9},{10,18},{18,10},{11,19},{19,11},{12,20... | collective-permute-start | bytes 2457608 | tf_op jit(solution)/shard_map/ppermute | solution.py:80
  328.8 8.0 %collective-permute-start.19 = (bf16[2,40,2560]{2,0,1:T(2,128)(2,1)S(1)}, bf16[2,40,2560]{2,0,1:T(2,128)(2,1)S(1)}, u32[]{:S(2)}, u32[]{:S(2)}) collective-permute-start(bf16[2,40,2560]{2,0,1:T(2,128)(2,1)S(1)} %pad_maximum_fusion.17), channel_id=1, source_target_pairs={{0,2},{1,3},{2,0},{3,1},{4,6},{5,7},{6,4},{7,5},{8,10},{9,11},{10,... | collective-permute-start | bytes 1228808 | tf_op jit(solution)/shard_map/ppermute | solution.py:25
  331.5 10.3 %collective-permute-start.21 = (bf16[2,41,2560]{2,0,1:T(2,128)(2,1)S(1)}, bf16[2,41,2560]{2,0,1:T(2,128)(2,1)S(1)}, u32[]{:S(2)}, u32[]{:S(2)}) collective-permute-start(bf16[2,41,2560]{2,0,1:T(2,128)(2,1)S(1)} %pad_maximum_fusion.16), channel_id=1, source_target_pairs={{0,4},{1,5},{2,6},{3,7},{4,0},{5,1},{6,2},{7,3},{8,12},{9,13},{10,... | collective-permute-start | bytes 1259528 | tf_op jit(solution)/shard_map/ppermute | solution.py:25
  349.5 13.1 %collective-permute-start.23 = (bf16[81,2560]{1,0:T(8,128)(2,1)S(1)}, bf16[81,2560]{1,0:T(8,128)(2,1)S(1)}, u32[]{:S(2)}, u32[]{:S(2)}) collective-permute-start(bf16[81,2560]{1,0:T(8,128)(2,1)S(1)} %pad_maximum_fusion.15), channel_id=1, source_target_pairs={{0,8},{24,16},{1,9},{25,17},{2,10},{26,18},{3,11},{27,19},{4,12},{... | collective-permute-start | bytes 1244168 | tf_op jit(solution)/shard_map/ppermute | solution.py:79
  357.9 22.4 %collective-permute-start.40 = (bf16[640,640]{1,0:T(8,128)(2,1)S(1)}, bf16[640,640]{1,0:T(8,128)(2,1)S(1)}, u32[]{:S(2)}, u32[]{:S(2)}) collective-permute-start(bf16[640,640]{1,0:T(8,128)(2,1)S(1)} %add_convert_fusion.2), channel_id=1, source_target_pairs={{8,0},{16,24},{9,1},{17,25},{10,2},{18,26},{11,3},{19,27},{12,4},{... | collective-permute-start | bytes 2457608 | tf_op jit(solution)/shard_map/ppermute | solution.py:81
  362.7 18.9 %collective-permute-start.24 = (bf16[81,2560]{1,0:T(8,128)(2,1)S(1)}, bf16[81,2560]{1,0:T(8,128)(2,1)S(1)}, u32[]{:S(2)}, u32[]{:S(2)}) collective-permute-start(bf16[81,2560]{1,0:T(8,128)(2,1)S(1)} %add_convert_fusion.8), channel_id=1, source_target_pairs={{8,16},{16,8},{9,17},{17,9},{10,18},{18,10},{11,19},{19,11},{12,20... | collective-permute-start | bytes 1244168 | tf_op jit(solution)/shard_map/ppermute | solution.py:80
  363.6 30.9 %collective-permute-start.33 = (bf16[80,5120]{1,0:T(8,128)(2,1)S(1)}, bf16[80,5120]{1,0:T(8,128)(2,1)S(1)}, u32[]{:S(2)}, u32[]{:S(2)}) collective-permute-start(bf16[80,5120]{1,0:T(8,128)(2,1)S(1)} %add_convert_fusion.4), channel_id=1, source_target_pairs={{8,0},{16,24},{9,1},{17,25},{10,2},{18,26},{11,3},{19,27},{12,4},{... | collective-permute-start | bytes 2457608 | tf_op jit(solution)/shard_map/ppermute | solution.py:81
  381.7 17.6 %collective-permute-start.25 = (bf16[81,2560]{1,0:T(8,128)(2,1)S(1)}, bf16[81,2560]{1,0:T(8,128)(2,1)S(1)}, u32[]{:S(2)}, u32[]{:S(2)}) collective-permute-start(bf16[81,2560]{1,0:T(8,128)(2,1)S(1)} %add_convert_fusion.7), channel_id=1, source_target_pairs={{8,0},{16,24},{9,1},{17,25},{10,2},{18,26},{11,3},{19,27},{12,4},{... | collective-permute-start | bytes 1244168 | tf_op jit(solution)/shard_map/ppermute | solution.py:81
  (81 other events, 1026.8 us)

commit v2 on v1

v2 whole, which is shorter than its diff:
```python
import functools
import math

import jax
import jax.numpy as jnp
from jax import lax
from jax.experimental import pallas as pl
from jax.experimental.pallas import tpu as pltpu
from jax.sharding import PartitionSpec as P

HEADS = 20
HEAD_DIM = 32
LANES = 128
SUBLANES = 8
SEGMENTS = 8
REACH = 192
CHUNK = 256
ROWS = 128
SCALE = 1.0 / math.sqrt(HEAD_DIM)
SCALE2 = math.log2(math.e) * SCALE
F32 = jnp.float32
BF16 = jnp.bfloat16
VECTORS = 8
ATTEND_GAIN, ATTEND_SHIFT, QUERY_BIAS, VALUE_BIAS = 0, 1, 2, 3
OUTPUT_BIAS, FORWARD_GAIN, FORWARD_SHIFT, DOWN_BIAS = 4, 5, 6, 7


def nn(left, right):
    return lax.dot_general(left, right, (((1,), (0,)), ((), ())), preferred_element_type=F32)


def nt(left, right):
    return lax.dot_general(left, right, (((1,), (1,)), ((), ())), preferred_element_type=F32)


def tn(left, right):
    return lax.dot_general(left, right, (((0,), (0,)), ((), ())), preferred_element_type=F32)


def call(kernel, outs, args, positions=None, grid=None, in_specs=None, out_specs=None, scratch=(),
         mib=16):
    whole = pl.BlockSpec(memory_space=pltpu.VMEM)
    in_specs = in_specs or [whole] * len(args)
    out_specs = out_specs or [whole] * len(outs)
    shapes = [jax.ShapeDtypeStruct(shape, dtype) for shape, dtype in outs]
    extra = [] if positions is None else [positions]
    return pl.pallas_call(
        kernel,
        out_shape=shapes,
        grid_spec=pltpu.PrefetchScalarGridSpec(
            num_scalar_prefetch=len(extra),
            grid=grid or (),
            in_specs=in_specs,
            out_specs=out_specs,
            scratch_shapes=list(scratch),
        ),
        compiler_params=pltpu.CompilerParams(vmem_limit_bytes=mib * 1024 * 1024),
        cost_estimate=pl.CostEstimate(flops=1, bytes_accessed=1, transcendentals=0),
    )(*extra, *args)


def unit(values):
    centred = values - jnp.mean(values, axis=-1, keepdims=True)
    spread = jnp.mean(centred * centred, axis=-1, keepdims=True)
    inverse = lax.rsqrt(spread + 1e-05)
    return centred * inverse, inverse


def unit_back(grad, normal, inverse, gain):
    scaled = grad * gain
    mean = jnp.mean(scaled, axis=-1, keepdims=True)
    along = jnp.mean(scaled * normal, axis=-1, keepdims=True)
    return inverse * (scaled - mean - normal * along)


def spans(length):
    chunk = min(CHUNK, length)
    return [
        (at, at + chunk, max(0, at - REACH), min(length, at + chunk + REACH))
        for at in range(0, length, chunk)
    ]


def split3(values):
    first = values.astype(BF16).astype(F32)
    rest = values - first
    second = rest.astype(BF16).astype(F32)
    return [first, second, rest - second]


def key_marks(segment_column):
    lane = lax.broadcasted_iota(jnp.int32, (segment_column.shape[0], LANES), 1)
    ones = (lane >= SEGMENTS) & (lane < SEGMENTS + 3)
    return jnp.where((lane == segment_column) | ones, 1.0, 0.0).astype(BF16)


def query_marks(segment_row):
    row = lax.broadcasted_iota(jnp.int32, (SEGMENTS, segment_row.shape[1]), 0)
    return jnp.where(row == segment_row, 0.0, -1e30)


def place(rows, head, marks):
    count = rows.shape[1]
    parts = [rows, marks, jnp.zeros((LANES - marks.shape[0], count), BF16)]
    if head < LANES // HEAD_DIM - 1:
        parts.insert(1, jnp.zeros((LANES - HEAD_DIM * (head + 1), count), BF16))
    if head:
        parts.insert(0, jnp.zeros((HEAD_DIM * head, count), BF16))
    return jnp.concatenate(parts, axis=0)


def attend_kernel(column_ref, row_ref, q_ref, k_ref, v_ref, out_ref, across_ref, lse_ref, marks_ref):
    @pl.when(pl.program_id(0) == 0)
    def _():
        marks_ref[...] = key_marks(column_ref[...])

    length = q_ref.shape[0]
    heads = LANES // HEAD_DIM
    queries = q_ref[...].T
    values = v_ref[...].T
    keys = jnp.concatenate([k_ref[...], marks_ref[...]], axis=1)
    blank = jnp.zeros((SUBLANES, length), F32)
    marks = jnp.concatenate([query_marks(row_ref[...]), blank], axis=0).astype(BF16)
    ones = jnp.ones((SUBLANES, length), BF16)
    bodies = [(head, span) for head in range(heads) for span in spans(length)]

    def rows(head):
        return slice(HEAD_DIM * head, HEAD_DIM * (head + 1))

    summed = [jnp.concatenate([values[rows(head)], ones], axis=0) for head in range(heads)]

    def score(head, span):
        begin, end, low, high = span
        return nn(keys[low:high], place(queries[rows(head), begin:end], head, marks[:, begin:end]))

    def finish(head, span, top, probs):
        begin, end, low, high = span
        out = nn(summed[head][:, low:high], probs)
        total = out[HEAD_DIM : HEAD_DIM + 1]
        across_ref[rows(head), begin:end] = out[:HEAD_DIM] * (1.0 / total)
        lse_ref[head : head + 1, begin:end] = (top + jnp.log2(total)) * (1.0 / SCALE2)

    scores = [score(*body) for body in bodies[:2]]
    waiting = None
    for at, body in enumerate(bodies):
        current = scores.pop(0)
        if at + 2 < len(bodies):
            scores.append(score(*bodies[at + 2]))
        top = jnp.max(current, axis=0, keepdims=True) * SCALE2
        probs = jnp.exp2(current * SCALE2 - top).astype(BF16)
        if waiting is not None:
            finish(*waiting)
        waiting = (*body, top, probs)
    finish(*waiting)
    lse_ref[heads:, :] = jnp.zeros((SUBLANES - heads, length), F32)
    out_ref[...] = across_ref[...].T.astype(BF16)


def attend_back_kernel(
    column_ref, row_ref, q_ref, k_ref, v_ref, grad_ref, across_ref, lse_ref,
    gq_ref, gk_ref, gv_ref, marks_ref, turned_ref,
):
    @pl.when(pl.program_id(0) == 0)
    def _():
        marks_ref[...] = key_marks(column_ref[...])

    length = q_ref.shape[0]
    grad = grad_ref[...]
    queries = q_ref[...].T
    turned_keys = k_ref[...].T
    grads = grad.T
    keys = jnp.concatenate([k_ref[...], marks_ref[...]], axis=1)
    values = jnp.concatenate([v_ref[...], marks_ref[...]], axis=1)
    low_marks = query_marks(row_ref[...])
    blank = jnp.zeros((SUBLANES, length), F32)
    lane = lax.broadcasted_iota(jnp.int32, (1, LANES), 1) // HEAD_DIM
    heads = []
    for head in range(LANES // HEAD_DIM):
        rows = slice(HEAD_DIM * head, HEAD_DIM * (head + 1))
        inner = jnp.sum(grads[rows].astype(F32) * across_ref[rows, :], axis=0, keepdims=True)
        lse = lse_ref[head : head + 1, :]
        score_marks = jnp.concatenate([low_marks, *split3(-lse), blank[:5]], axis=0)
        inner_marks = jnp.concatenate([blank, *split3(-inner), blank[:5]], axis=0)
        zero = jnp.zeros_like(grad)
        heads.append(
            (
                rows,
                score_marks.astype(BF16),
                inner_marks.astype(BF16),
                jnp.where(lane == head, q_ref[...], zero),
                jnp.where(lane == head, grad, zero),
            )
        )
    bodies = [
        (head, at, span) for head in range(len(heads)) for at, span in enumerate(spans(length))
    ]
    sums = [[None, None] for _ in spans(length)]

    def pair(head, at, span):
        begin, end, low, high = span
        rows, score_marks, inner_marks, _, _ = heads[head]
        return (
            nn(keys[low:high], place(queries[rows, begin:end], head, score_marks[:, begin:end])),
            nn(values[low:high], place(grads[rows, begin:end], head, inner_marks[:, begin:end])),
        )

    def finish(head, at, span, score_grads, probs):
        begin, end, low, high = span
        rows, _, _, own_queries, own_grads = heads[head]
        for which, (left, right) in enumerate(
            ((score_grads, own_queries[begin:end]), (probs, own_grads[begin:end]))
        ):
            part = nn(left, right)
            sums[at][which] = part if sums[at][which] is None else sums[at][which] + part
        turned_ref[rows, begin:end] = nn(turned_keys[rows, low:high], score_grads)

    ahead = [pair(*bodies[0])]
    waiting = None
    for at, body in enumerate(bodies):
        scores, differences = ahead.pop(0)
        if at + 1 < len(bodies):
            ahead.append(pair(*bodies[at + 1]))
        probs = jnp.exp2(scores * SCALE2)
        score_grads = (probs * differences).astype(BF16)
        if waiting is not None:
            finish(*waiting)
        waiting = (*body, score_grads, probs.astype(BF16))
    finish(*waiting)
    gq_ref[...] = (turned_ref[...].T * SCALE).astype(BF16)
    for which, (ref, factor) in enumerate(((gk_ref, SCALE), (gv_ref, 1.0))):
        total = None
        for at, (_, _, low, high) in enumerate(spans(length)):
            parts = [sums[at][which]]
            if low:
                parts.insert(0, jnp.zeros((low, LANES), F32))
            if high < length:
                parts.append(jnp.zeros((length - high, LANES), F32))
            part = jnp.concatenate(parts, axis=0) if len(parts) > 1 else parts[0]
            total = part if total is None else total + part
        ref[...] = (total * factor).astype(BF16)


def attention_specs(length, width):
    tiles = width // LANES

    def tile(at):
        return pl.BlockSpec((length, LANES), lambda i: (0, at + i))

    return (
        tiles,
        tile,
        pl.BlockSpec((length, 1), lambda i: (0, 0)),
        pl.BlockSpec((1, length), lambda i: (0, 0)),
        pl.BlockSpec((LANES, length), lambda i: (i, 0)),
        pl.BlockSpec((SUBLANES, length), lambda i: (i, 0)),
    )


def attend(joined, column, row):
    length = joined.shape[0]
    width = joined.shape[1] // 3
    tiles, tile, column_spec, row_spec, across_spec, lse_spec = attention_specs(length, width)
    return call(
        attend_kernel,
        [((length, width), BF16), ((width, length), F32), ((SUBLANES * tiles, length), F32)],
        (column, row, joined, joined, joined),
        grid=(tiles,),
        in_specs=[column_spec, row_spec, tile(0), tile(tiles), tile(2 * tiles)],
        out_specs=[tile(0), across_spec, lse_spec],
        scratch=[pltpu.VMEM((length, LANES), BF16)],
    )


def attend_back(joined, column, row, grad, across, lse):
    length = joined.shape[0]
    width = joined.shape[1] // 3
    tiles, tile, column_spec, row_spec, across_spec, lse_spec = attention_specs(length, width)
    return call(
        attend_back_kernel,
        [((length, width), BF16)] * 3,
        (column, row, joined, joined, joined, grad, across, lse),
        grid=(tiles,),
        in_specs=[column_spec, row_spec, tile(0), tile(tiles), tile(2 * tiles), tile(0), across_spec, lse_spec],
        out_specs=[tile(0)] * 3,
        scratch=[pltpu.VMEM((length, LANES), BF16), pltpu.VMEM((LANES, length), F32)],
        mib=24,
    )


def slab_kernel(heads_ref, out_ref, short_ref, up_ref, slab_ref):
    rows = heads_ref.shape[0]
    width = out_ref.shape[1]
    slab_ref[:rows, : 3 * width] = heads_ref[...]
    slab_ref[:rows, 3 * width :] = out_ref[...]
    slab_ref[rows:, :] = jnp.zeros((VECTORS, 4 * width), BF16)
    slab_ref[rows:, :rows] = short_ref[...]
    slab_ref[rows:, LANES : LANES + up_ref.shape[1]] = jnp.broadcast_to(
        up_ref[...], (VECTORS, up_ref.shape[1])
    )


def halves_kernel(hidden, position_ref, up_ref, mine_ref, other_ref):
    for at in range(mine_ref.shape[1] // hidden):
        here = slice(hidden * at, hidden * (at + 1))
        for core, ref in enumerate((mine_ref, other_ref)):
            begin = (2 * at + (position_ref[0] + core) % 2) * hidden
            ref[:, here] = up_ref[:, pl.ds(pl.multiple_of(begin, LANES), hidden)]


def project_kernel(count, rows, hidden, position_ref, x_ref, *refs):
    slabs, refs = refs[:count], refs[count:]
    length, width = x_ref.shape
    if count:
        low_ref, joined_ref, heads_ref, out_ref, vector_ref, bias_ref, short_ref, sems = refs
        copies = []
        for at, slab in enumerate(slabs):
            begin = pl.multiple_of(position_ref[at] * rows, SUBLANES)
            here = pl.ds(begin, rows)
            for which, (source, target) in enumerate(
                (
                    (slab.at[pl.ds(0, rows), pl.ds(0, 3 * width)], heads_ref.at[here]),
                    (slab.at[pl.ds(0, rows), pl.ds(3 * width, width)], out_ref.at[here]),
                    (slab.at[pl.ds(rows, VECTORS), pl.ds(0, LANES + hidden)], short_ref.at[at]),
                )
            ):
                copy = pltpu.make_async_copy(source, target, sems.at[at, which])
                copy.start()
                copies.append(copy)
    else:
        heads_ref, vector_ref, low_ref, joined_ref = refs
    if count:
        for copy in copies:
            copy.wait()
        vectors = jnp.zeros((VECTORS, width), F32)
        for at in range(count):
            begin = position_ref[at] * rows
            short = short_ref[at, :, :LANES].astype(F32)
            lane = lax.broadcasted_iota(jnp.int32, short.shape, 1)
            short = jnp.where(lane < rows, short, 0.0)
            short = jnp.concatenate([short, jnp.zeros((VECTORS, width - LANES), F32)], axis=1)
            vectors = vectors + pltpu.roll(short, begin, 1)
            if at < count // 2:
                begin = pl.multiple_of(lax.div(position_ref[at], 2) * hidden, LANES)
                bias_ref[:, pl.ds(begin, hidden)] = short_ref[at, :, LANES:].astype(F32)
        vector_ref[...] = vectors
    zero = jnp.zeros((1, width), F32)
    vector = vector_ref[...]
    bias = jnp.concatenate(
        [vector[QUERY_BIAS : QUERY_BIAS + 1], zero, vector[VALUE_BIAS : VALUE_BIAS + 1]], axis=1
    )
    for at in range(0, length, ROWS):
        normal, _ = unit(x_ref[at : at + ROWS, :].astype(F32))
        low_ref[at : at + ROWS, :] = (
            normal * vector[ATTEND_GAIN : ATTEND_GAIN + 1]
            + vector[ATTEND_SHIFT : ATTEND_SHIFT + 1]
        ).astype(BF16)
    for at in range(0, 3 * width, width):
        here = slice(at, at + width)
        joined_ref[:, here] = (nn(low_ref[...], heads_ref[:, here]) + bias[:, here]).astype(BF16)


def middle_kernel(x_ref, attended_ref, out_ref, vector_ref, middle_ref, low_ref):
    vector = vector_ref[...]
    for at in range(0, x_ref.shape[0], ROWS):
        here = slice(at, at + ROWS)
        middle = (
            x_ref[here, :].astype(F32)
            + nn(attended_ref[here, :], out_ref[...])
            + vector[OUTPUT_BIAS : OUTPUT_BIAS + 1]
        )
        middle_ref[here, :] = middle
        normal, _ = unit(middle)
        low_ref[here, :] = (
            normal * vector[FORWARD_GAIN : FORWARD_GAIN + 1]
            + vector[FORWARD_SHIFT : FORWARD_SHIFT + 1]
        ).astype(BF16)


def up_kernel(position_ref, own_ref, other_ref, bias_ref, *refs):
    parts, (act_ref, slope_ref, full_ref) = refs[: len(refs) - 3], refs[len(refs) - 3 :]
    for at, part in enumerate(parts):
        rows = part.shape[0]
        begin = pl.multiple_of(position_ref[at] * rows, SUBLANES)
        full_ref[pl.ds(begin, rows), :] = part[...]
    weight = full_ref[...]
    bias = bias_ref[:1, :]
    length = own_ref.shape[0]
    for which, ref in enumerate((own_ref, other_ref)):
        for at in range(0, length, ROWS):
            upward = nn(ref[at : at + ROWS, :], weight) + bias
            share = 0.5 + 0.5 * lax.erf(upward * math.sqrt(0.5))
            bell = jnp.exp2((upward * upward) * (-0.5 * math.log2(math.e)))
            here = slice(which * length + at, which * length + at + ROWS)
            act_ref[here, :] = (upward * share).astype(BF16)
            slope = share + upward * (bell * (1.0 / math.sqrt(2.0 * math.pi)))
            slope_ref[here, :] = slope.astype(BF16)


def column_specs(half, block):
    block = min(block, half)

    def column(height):
        return pl.BlockSpec((height, block), lambda i, at: (0, i))

    return half // block, block, column


def whole_spec(shape):
    return pl.BlockSpec(shape, lambda i, at: (0,) * len(shape))


def up_project(own, other, bias, parts, positions):
    length, width = own.shape
    half = parts[0].shape[1]
    steps, _, column = column_specs(half, 512)
    whole = whole_spec((length, width))
    return call(
        up_kernel,
        [((2 * length, half), BF16), ((2 * length, half), BF16), ((width, half), BF16)],
        (own, other, bias, *parts),
        positions,
        grid=(steps,),
        in_specs=[whole, whole, column(bias.shape[0])] + [column(part.shape[0]) for part in parts],
        out_specs=[column(2 * length), column(2 * length), column(width)],
    )


def down_kernel(position_ref, act_ref, *refs):
    parts, (own_ref, other_ref, full_ref) = refs[: len(refs) - 3], refs[len(refs) - 3 :]
    length = own_ref.shape[0]
    for at, part in enumerate(parts):
        rows = part.shape[0]
        begin = pl.multiple_of(position_ref[at] * rows, SUBLANES)
        full_ref[pl.ds(begin, rows), :] = part[...]
    for which, ref in enumerate((own_ref, other_ref)):
        here = slice(which * length, (which + 1) * length)
        ref[...] = nn(act_ref[here, :], full_ref[...]).astype(ref.dtype)


def down_project(act, parts, positions):
    length = act.shape[0] // 2
    half = act.shape[1]
    width = parts[0].shape[1]
    return call(
        down_kernel,
        [((length, width), F32), ((length, width), BF16), ((half, width), BF16)],
        (act, *parts),
        positions,
        mib=20,
    )


def loss_kernel(
    middle_ref, own_ref, got_ref, vector_ref, readout_ref, target_ref, mask_ref,
    low_ref, down_ref, grad_ref, lanes_ref, sums_ref,
):
    result = (
        middle_ref[...]
        + (own_ref[...] + got_ref[...].astype(F32))
        + vector_ref[DOWN_BIAS : DOWN_BIAS + 1, :]
    ).astype(BF16)
    low_ref[...] = result
    logits = nt(readout_ref[...], result)
    length = logits.shape[1]
    top = jnp.max(logits, axis=0, keepdims=True)
    shifted = jnp.exp(logits - top)
    total = jnp.sum(shifted, axis=0, keepdims=True)
    onehot = lax.broadcasted_iota(jnp.int32, logits.shape, 0) == target_ref[...]
    picked = jnp.sum(jnp.where(onehot, logits, 0.0), axis=0, keepdims=True)
    weight = mask_ref[...].astype(F32)
    loss = (top + jnp.log(total) - picked) * weight
    loss_lanes = jnp.zeros((1, LANES), F32)
    count_lanes = jnp.zeros((1, LANES), F32)
    for at in range(0, length, LANES):
        loss_lanes = loss_lanes + loss[:, at : at + LANES]
        count_lanes = count_lanes + weight[:, at : at + LANES]
    blank = jnp.zeros((SUBLANES - 2, LANES), F32)
    lanes_ref[...] = jnp.concatenate([loss_lanes, count_lanes, blank], axis=0)
    grad_logits = (weight * (shifted / total - onehot.astype(F32))).astype(BF16)
    grad = tn(grad_logits, readout_ref[...])
    grad_ref[...] = grad
    low = grad.astype(BF16)
    down_ref[...] = low
    sums_ref[...] = jnp.sum(low.astype(F32), axis=0, keepdims=True)


def down_grad_kernel(chips, position_ref, act_ref, own_ref, other_ref, *out_refs):
    length = own_ref.shape[0]
    hidden = act_ref.shape[1] // chips
    for offset in range(chips):
        if len(out_refs) == 1:
            begin = offset * hidden
        else:
            begin = pl.multiple_of((position_ref[0] ^ offset) * hidden, LANES)
        here = pl.ds(begin, hidden)
        part = tn(act_ref[:length, here], own_ref[...]) + tn(act_ref[length:, here], other_ref[...])
        part = part.astype(BF16)
        if len(out_refs) == 1:
            out_refs[0][begin : begin + hidden, :] = part
            continue
        keep_x, send_x, keep_y, send_y = out_refs
        half = hidden // 2
        (send_x if offset % 2 else keep_x)[offset // 2, :, :] = part[:half]
        (send_y if offset // 2 else keep_y)[offset % 2, :, :] = part[half:]


def down_grad(act, own, other, chips, position):
    half = act.shape[1]
    width = own.shape[1]
    if square():
        outs = [((2, half // chips // 2, width), BF16)] * 4
    else:
        outs = [((half, width), BF16)]
    return call(
        functools.partial(down_grad_kernel, chips), outs, (act, own, other), position, mib=20
    )


def up_grad_kernel(
    rows, position_ref, own_ref, other_ref, slope_ref, second_ref, second_other_ref, down_ref,
    up_ref, bias_ref, *refs,
):
    out_refs, part_ref = refs[:-1], refs[-1]
    length = own_ref.shape[0]
    total = None
    grads = []
    for which, ref in enumerate((own_ref, other_ref)):
        for at in range(0, length, 2 * ROWS):
            here = slice(which * length + at, which * length + at + 2 * ROWS)
            grad = nt(ref[at : at + 2 * ROWS, :], down_ref[...]) * slope_ref[here, :].astype(F32)
            low = grad.astype(BF16)
            up_ref[here, :] = low
            part = jnp.sum(low.astype(F32), axis=0, keepdims=True)
            total = part if total is None else total + part
    bias_ref[...] = total
    part = tn(second_ref[...], up_ref[:length, :]) + tn(second_other_ref[...], up_ref[length:, :])
    if len(out_refs) == 1:
        out_refs[0][...] = part.astype(BF16)
        return
    part_ref[...] = part
    keep_x, send_x, keep_y, send_y = out_refs
    for offset in range(4):
        begin = pl.multiple_of((position_ref[0] ^ offset) * (2 * rows), SUBLANES)
        upper = part_ref[pl.ds(begin, rows), :].astype(BF16)
        lower = part_ref[pl.ds(begin + rows, rows), :].astype(BF16)
        (send_x if offset % 2 else keep_x)[offset // 2, :, :] = upper
        (send_y if offset // 2 else keep_y)[offset % 2, :, :] = lower


def up_grad(own, other, slope, second, second_other, down_full, rows, position):
    length, width = own.shape
    half = slope.shape[1]
    steps, block, column = column_specs(half, 512)
    whole = whole_spec((length, width))
    if square():
        outs = [((2, rows, half), BF16)] * 4
        specs = [pl.BlockSpec((2, rows, block), lambda i, at: (0, 0, i))] * 4
    else:
        outs = [((width, half), BF16)]
        specs = [column(width)]
    return call(
        functools.partial(up_grad_kernel, rows),
        [((2 * length, half), BF16), ((1, half), F32), *outs],
        (own, other, slope, second, second_other, down_full),
        position,
        grid=(steps,),
        in_specs=[
            whole, whole, column(2 * length), whole, whole,
            pl.BlockSpec((block, width), lambda i, at: (i, 0)),
        ],
        out_specs=[column(2 * length), column(1), *specs],
        scratch=[pltpu.VMEM((width, block), F32)],
        mib=20,
    )


def inward_kernel(grad_ref, up_ref, own_ref, other_ref):
    length = own_ref.shape[0]
    other_ref[...] = nt(grad_ref[length:, :], up_ref[...]).astype(BF16)
    own_ref[...] = nt(grad_ref[:length, :], up_ref[...])


def join_kernel(hidden, position_ref, mine_ref, other_ref, out_ref):
    for at in range(mine_ref.shape[1] // hidden):
        here = slice(hidden * at, hidden * (at + 1))
        for core, ref in enumerate((mine_ref, other_ref)):
            begin = (2 * at + (position_ref[0] + core) % 2) * hidden
            out_ref[:, pl.ds(pl.multiple_of(begin, LANES), hidden)] = ref[:, here].astype(F32)


def branch_kernel(
    own_ref, got_ref, middle_ref, result_ref, out_ref, vector_ref,
    grad_ref, branch_ref, attended_ref, sums_ref,
):
    width = own_ref.shape[1]
    gain = vector_ref[FORWARD_GAIN : FORWARD_GAIN + 1, :]
    sums = [jnp.zeros((1, width), F32) for _ in range(3)]
    for at in range(0, own_ref.shape[0], ROWS):
        here = slice(at, at + ROWS)
        grad = own_ref[here, :] + got_ref[here, :].astype(F32)
        normal, inverse = unit(middle_ref[here, :])
        middle = result_ref[here, :] + unit_back(grad, normal, inverse, gain)
        grad_ref[here, :] = middle
        branch = middle.astype(BF16)
        branch_ref[here, :] = branch
        attended_ref[here, :] = nt(branch, out_ref[...]).astype(BF16)
        for which, part in enumerate((grad * normal, grad, branch.astype(F32))):
            sums[which] = sums[which] + jnp.sum(part, axis=0, keepdims=True)
    blank = jnp.zeros((SUBLANES - 3, width), F32)
    sums_ref[...] = jnp.concatenate([*sums, blank], axis=0)


def last_kernel(
    count, rows, hidden, position_ref,
    x_ref, low_ref, gq_ref, gk_ref, gv_ref, heads_ref, attended_ref, branch_ref, grad_ref,
    vector_ref, sums_ref, down_ref, up_ref, lanes_ref, *refs,
):
    slabs, (input_ref, vectors_ref, full_ref) = refs[:count], refs[count:]
    width = x_ref.shape[1]
    for at, ref in enumerate((gq_ref, gk_ref, gv_ref)):
        part = tn(low_ref[...], ref[...])
        full_ref[:, width * at : width * (at + 1)] = part.astype(BF16)
    full_ref[:, 3 * width :] = tn(attended_ref[...], branch_ref[...]).astype(BF16)
    gain = vector_ref[ATTEND_GAIN : ATTEND_GAIN + 1, :]
    sums = [jnp.zeros((1, width), F32) for _ in range(4)]
    for at in range(0, x_ref.shape[0], ROWS):
        here = slice(at, at + ROWS)
        grad = (
            nt(gq_ref[here, :], heads_ref[:, :width])
            + nt(gk_ref[here, :], heads_ref[:, width : 2 * width])
            + nt(gv_ref[here, :], heads_ref[:, 2 * width :])
        )
        normal, inverse = unit(x_ref[here, :].astype(F32))
        input_ref[here, :] = grad_ref[here, :] + unit_back(grad, normal, inverse, gain)
        parts = (grad * normal, grad, gq_ref[here, :].astype(F32), gv_ref[here, :].astype(F32))
        for which, part in enumerate(parts):
            sums[which] = sums[which] + jnp.sum(part, axis=0, keepdims=True)
    vectors = jnp.concatenate(
        [*sums, sums_ref[2:3, :], sums_ref[0:1, :], sums_ref[1:2, :], down_ref[...]], axis=0
    )
    vectors_ref[...] = vectors
    blank = jnp.zeros((VECTORS - 1, hidden), F32)
    for at, slab in enumerate(slabs):
        place_at = position_ref[at]
        begin = pl.multiple_of(place_at * rows, SUBLANES)
        slab[:rows, :] = full_ref[pl.ds(begin, rows), :]
        short = pltpu.roll(vectors, width - begin, 1)[:, :LANES]
        if at < count // 2:
            hidden_at = pl.multiple_of(lax.div(place_at, 2) * hidden, LANES)
            bias = jnp.concatenate([up_ref[:, pl.ds(hidden_at, hidden)], blank], axis=0)
        else:
            bias = jnp.zeros((VECTORS, hidden), F32)
        row = jnp.concatenate([short, bias, lanes_ref[...]], axis=1).astype(BF16)
        pad = jnp.zeros((VECTORS, 4 * width - row.shape[1]), BF16)
        slab[rows:, :] = jnp.concatenate([row, pad], axis=1)


def swap(values, bit):
    return lax.ppermute(values, "wide", [(i, i ^ bit) for i in range(lax.axis_size("wide"))])


def same_core_groups():
    chips = lax.axis_size("wide") // 2
    return [[2 * chip + core for chip in range(chips)] for core in range(2)]


def square():
    return lax.axis_size("wide") == 8


def spread_chips(shard):
    return lax.all_gather(shard, "wide", axis=0, axis_index_groups=same_core_groups())


def add_low(*parts):
    return sum(part.astype(F32) for part in parts).astype(BF16)


def collect_chips(parts):
    return lax.psum_scatter(
        parts, "wide", scatter_dimension=0, axis_index_groups=same_core_groups()
    )


def collect_square(keep_x, send_x, keep_y, send_y):
    from_x = swap(send_x, 2)
    from_y = swap(send_y, 4)
    upper = swap(add_low(keep_x[1], from_x[1]), 4)
    lower = swap(add_low(keep_y[1], from_y[1]), 2)
    return add_low(keep_x[0], from_x[0], upper), add_low(keep_y[0], from_y[0], lower)


def sum_narrow(shard):
    if lax.axis_size("narrow") != 4:
        return lax.psum(shard, "narrow")
    place_at = lax.axis_index("narrow")
    inner = (place_at == 1) | (place_at == 2)
    half = add_low(shard, lax.ppermute(shard, "narrow", [(0, 1), (3, 2)]))
    total = add_low(half, lax.ppermute(half, "narrow", [(1, 2), (2, 1)]))
    outer = lax.ppermute(total, "narrow", [(1, 0), (2, 3)])
    return jnp.where(inner, total, outer)


def local(
    layer_input, segments, targets, loss_mask, readout,
    attend_gain, attend_shift, heads_weight, query_bias, value_bias, output_weight, output_bias,
    forward_gain, forward_shift, up_weight, up_bias, down_weight, down_bias,
):
    length = layer_input.shape[1]
    width = layer_input.shape[2]
    wide = lax.axis_size("wide")
    chips = wide // 2
    core = lax.axis_index("wide") % 2
    chip = lax.axis_index("wide") // 2
    rows = heads_weight.shape[0]
    hidden = up_bias.shape[0]
    half = chips * hidden
    x = layer_input[0]
    column = segments.reshape(length, 1)

    def by_core(mine, other, axis):
        return jnp.where(
            core == 0, jnp.stack([mine, other], axis), jnp.stack([other, mine], axis)
        )

    def mine_of(values, axis, flip=0):
        return lax.dynamic_index_in_dim(values, core ^ flip, axis, keepdims=False)

    short = jnp.stack(
        [
            attend_gain, attend_shift, query_bias, value_bias,
            output_bias, forward_gain, forward_shift, down_bias,
        ]
    )
    core_position = core.reshape(1).astype(jnp.int32)
    chip_position = chip.reshape(1).astype(jnp.int32)
    if square():
        offsets = jnp.arange(4, dtype=jnp.int32)
        (slab,) = call(
            slab_kernel,
            [((rows + VECTORS, 4 * width), BF16)],
            (heads_weight, output_weight, short, up_bias[None]),
        )
        slabs = [slab, swap(slab, 2), swap(slab, 4), swap(slab, 6)]
        slabs = slabs + [swap(part, 1) for part in slabs]
        devices = 2 * (chip ^ offsets) + core
        positions = jnp.concatenate([devices, devices ^ 1]).astype(jnp.int32)
        first_low, joined, heads_full, output_full, vectors, up_bias_half = call(
            functools.partial(project_kernel, len(slabs), rows, hidden),
            [
                ((length, width), BF16), ((length, 3 * width), BF16), ((width, 3 * width), BF16),
                ((width, width), BF16), ((VECTORS, width), F32), ((VECTORS, half), F32),
            ],
            (x, *slabs),
            positions,
            in_specs=[pl.BlockSpec(memory_space=pltpu.VMEM)]
            + [pl.BlockSpec(memory_space=pl.ANY)] * len(slabs),
            scratch=[
                pltpu.VMEM((len(slabs), VECTORS, LANES + hidden), BF16),
                pltpu.SemaphoreType.DMA((len(slabs), 3)),
            ],
            mib=20,
        )
        up_mine, up_other = call(
            functools.partial(halves_kernel, hidden),
            [((rows, half), BF16)] * 2,
            (up_weight,),
            core_position,
        )
        mine_x, other_x = swap(up_mine, 2), swap(up_other, 3)
        mine_y, other_y = swap(up_mine, 4), swap(up_other, 5)
        up_parts = [
            up_mine, mine_x, mine_y, swap(mine_y, 2),
            swap(up_other, 1), other_x, other_y, swap(other_x, 4),
        ]
        down_x, down_y = swap(down_weight, 2), swap(down_weight, 4)
        middle_row = hidden // 2
        down_parts = [
            down_weight, down_x, down_y,
            swap(down_y[:middle_row], 2), swap(down_x[middle_row:], 4),
        ]
        up_positions = positions
        chip_at = chip ^ offsets
        down_positions = jnp.concatenate(
            [chip_at[:3], 2 * chip_at[3:], 2 * chip_at[3:] + 1]
        ).astype(jnp.int32)
    else:
        tail = jnp.concatenate([short.reshape(1, 8 * rows), up_bias[None]], axis=1)
        tail = jnp.pad(tail, ((0, 0), (0, 4 * width - tail.shape[1])))
        slab = jnp.concatenate(
            [jnp.concatenate([heads_weight, output_weight], axis=1), tail], axis=0
        )
        slabs = lax.all_gather(slab, "wide", axis=0)
        attend_full = slabs[:, :rows].reshape(width, 4 * width)
        heads_full = attend_full[:, : 3 * width]
        output_full = attend_full[:, 3 * width :]
        last = slabs[:, rows].astype(F32)
        vectors = last[:, : 8 * rows].reshape(wide, 8, rows).transpose(1, 0, 2).reshape(8, width)
        up_bias_half = mine_of(last[:, 8 * rows : 8 * rows + hidden].reshape(chips, 2, hidden), 1)
        up_bias_half = jnp.broadcast_to(up_bias_half.reshape(1, half), (VECTORS, half))
        positions = jnp.zeros((1,), jnp.int32)
        first_low, joined = call(
            functools.partial(project_kernel, 0, rows, hidden),
            [((length, width), BF16), ((length, 3 * width), BF16)],
            (x, heads_full, vectors),
            positions,
            mib=20,
        )
        up_view = up_weight.reshape(rows, chips, 2, hidden)
        up_pair = by_core(
            mine_of(up_view, 2).reshape(rows, half),
            swap(mine_of(up_view, 2, 1).reshape(rows, half), 1),
            0,
        ).reshape(2 * rows, half)
        up_parts = [spread_chips(up_pair).reshape(width, half)]
        down_parts = [spread_chips(down_weight).reshape(half, width)]
        up_positions = down_positions = positions

    attended, across, lse = attend(joined, column, segments)
    middle, second_low = call(
        middle_kernel,
        [((length, width), F32), ((length, width), BF16)],
        (x, attended, output_full, vectors),
    )

    second_other = swap(second_low, 1)
    activated, slope, up_full = up_project(
        second_low, second_other, up_bias_half, up_parts, up_positions
    )
    outward, outward_other, down_full = down_project(activated, down_parts, down_positions)
    result_low, grad_down, grad_result, lanes, down_bias_part = call(
        loss_kernel,
        [
            ((length, width), BF16), ((length, width), BF16), ((length, width), F32),
            ((SUBLANES, LANES), F32), ((1, width), F32),
        ],
        (middle, outward, swap(outward_other, 1), vectors, readout.T, targets, loss_mask),
    )

    grad_down_other = swap(grad_down, 1)
    down_parts = down_grad(activated, grad_down, grad_down_other, chips, chip_position)
    grad_up, up_bias_part, *up_parts = up_grad(
        grad_down, grad_down_other, slope, second_low, second_other, down_full, rows, chip_position
    )
    inward, inward_other = call(
        inward_kernel,
        [((length, width), F32), ((length, width), BF16)],
        (grad_up, up_full),
        mib=20,
    )
    grad_middle, grad_branch, grad_attended, branch_sums = call(
        branch_kernel,
        [
            ((length, width), F32), ((length, width), BF16), ((length, width), BF16),
            ((SUBLANES, width), F32),
        ],
        (inward, swap(inward_other, 1), middle, grad_result, output_full, vectors),
    )
    if square():
        down_sums = [sum_narrow(part) for part in collect_square(*down_parts)]
        down_weight_sum = jnp.concatenate(down_sums).astype(F32)
        upper, lower = [sum_narrow(part) for part in collect_square(*up_parts)]
        first = core == 0
        (up_weight_sum,) = call(
            functools.partial(join_kernel, hidden),
            [((rows, 2 * half), F32)],
            (jnp.where(first, upper, lower), swap(jnp.where(first, lower, upper), 1)),
            core_position,
        )
    else:
        down_weight_sum = collect_chips(down_parts[0].reshape(chips, hidden, width))
        down_weight_sum = sum_narrow(down_weight_sum).astype(F32)
        up_sum = sum_narrow(collect_chips(up_parts[0].reshape(chips, 2 * rows, half)))
        up_sum = up_sum.reshape(2, rows, chips, hidden)
        up_weight_sum = by_core(mine_of(up_sum, 0), swap(mine_of(up_sum, 0, 1), 1), 2)
        up_weight_sum = up_weight_sum.reshape(rows, 2 * half).astype(F32)

    grad_query, grad_key, grad_value = attend_back(
        joined, column, segments, grad_attended, across, lse
    )
    slab_shape = ((rows + VECTORS, 4 * width), BF16)
    *slabs, input_grad, short_sums, attend_part = call(
        functools.partial(last_kernel, 8 if square() else 0, rows, hidden),
        ([slab_shape] * 8 if square() else [])
        + [((length, width), F32), ((VECTORS, width), F32), ((width, 4 * width), BF16)],
        (
            x, first_low, grad_query, grad_key, grad_value, heads_full, attended, grad_branch,
            grad_middle, vectors, branch_sums, down_bias_part, up_bias_part, lanes,
        ),
        positions,
        mib=40,
    )
    if square():
        both = [add_low(slabs[at], swap(slabs[4 + at], 1)) for at in (3, 1, 2, 0)]
        got = [swap(both[0], 6), swap(both[1], 2), swap(both[2], 4)]
        slab = sum_narrow(add_low(both[3], *got)).astype(F32)
        vectors_sum = slab[rows:, :rows]
        up_bias_grad = slab[rows, LANES : LANES + hidden]
        lanes_sum = slab[rows : rows + 2, LANES + hidden : 2 * LANES + hidden]
    else:
        short = short_sums.reshape(8, wide, rows).transpose(1, 0, 2).reshape(wide, 8 * rows)
        up_bias_rows = up_bias_part.reshape(chips, hidden)
        up_bias_rows = by_core(up_bias_rows, jnp.zeros_like(up_bias_rows), 1).reshape(wide, hidden)
        shared = jnp.broadcast_to(lanes[:2].reshape(1, 2 * LANES), (wide, 2 * LANES))
        row = jnp.concatenate([short, up_bias_rows, shared], axis=1).astype(BF16)
        row = jnp.pad(row, ((0, 0), (0, 4 * width - row.shape[1])))
        slab = jnp.concatenate([attend_part.reshape(wide, rows, 4 * width), row[:, None]], axis=1)
        slab = sum_narrow(lax.psum_scatter(slab, "wide", scatter_dimension=0)).astype(F32)
        vectors_sum = slab[rows, : 8 * rows].reshape(8, rows)
        up_bias_grad = slab[rows, 8 * rows : 8 * rows + hidden]
        lanes_sum = slab[rows, 8 * rows + hidden : 8 * rows + hidden + 2 * LANES].reshape(2, LANES)
    return (
        result_low[None],
        input_grad[None],
        vectors_sum[ATTEND_GAIN],
        vectors_sum[ATTEND_SHIFT],
        slab[:rows, : 3 * width],
        vectors_sum[QUERY_BIAS],
        vectors_sum[VALUE_BIAS],
        slab[:rows, 3 * width :],
        vectors_sum[OUTPUT_BIAS],
        vectors_sum[FORWARD_GAIN],
        vectors_sum[FORWARD_SHIFT],
        up_weight_sum,
        up_bias_grad,
        down_weight_sum,
        vectors_sum[DOWN_BIAS],
        jnp.sum(lanes_sum[0]),
        jnp.round(jnp.sum(lanes_sum[1])).astype(jnp.int32),
    )


def solution(mesh):
    in_specs = (
        P(("narrow", "wide"), None, None),
        P(("narrow", "wide"), None),
        P(("narrow", "wide"), None),
        P(("narrow", "wide"), None),
        P(),
        P("wide"),
        P("wide"),
        P("wide", None),
        P("wide"),
        P("wide"),
        P("wide", None),
        P("wide"),
        P("wide"),
        P("wide"),
        P("wide", None),
        P("wide"),
        P("wide", None),
        P("wide"),
    )
    out_specs = (
        P(("narrow", "wide"), None, None),
        P(("narrow", "wide"), None, None),
        P("wide"),
        P("wide"),
        P("wide", None),
        P("wide"),
        P("wide"),
        P("wide", None),
        P("wide"),
        P("wide"),
        P("wide"),
        P("wide", None),
        P("wide"),
        P("wide", None),
        P("wide"),
        P(),
        P(),
    )
    return jax.shard_map(local, mesh=mesh, in_specs=in_specs, out_specs=out_specs, check_vma=False)
```

time: 413 us -> 292 us (0.71); the launches traced: 405 us -> 291 us
  matrix products: 112 us -> 0 us
  Pallas kernels: 0 us -> 77.7 us
  other arithmetic: 71.7 us -> 9.13 us
  waiting for transfers between devices: 75 us -> 115 us
  local copies, waits for them, and re-layouts: 69.5 us -> 31.1 us
  blocking collectives: 24.6 us -> 0 us
  starting transfers between devices: 48 us -> 54.2 us
    dot_general x20 -> x0, matrix products: 112 us -> none  [the longest x1 28.2 us: local(): jnp.dot(second_both, up_half, preferred_element_type=jnp.float32)]
    pallas_call x0 -> x15, Pallas kernels: none -> 77.7 us  [call(): pl.pallas_call(kernel, out_shape=shapes, grid_spec=pltpu.PrefetchScalarGr...]
    convert_element_type x22 -> x24, other arithmetic: 33.2 us -> 8.16 us  [the longest x22 6.82 us: add_low(): return sum((part.astype(F32) for part in parts)).astype(BF16)]
    all_gather x1 -> x0, blocking collectives: 24.6 us -> none  [local(): lax.all_gather(jnp.concatenate([attend_gain, attend_shift, query_bias, va...]
    ppermute x32 -> x38, waiting for transfers between devices: 37.5 us -> 53.3 us  [swap(): lax.ppermute(values, 'wide', [(i, i ^ bit) for i in range(lax.axis_size('...]
    ppermute x3 -> x5, waiting for transfers between devices: 7.02 us -> 22.4 us  [sum_narrow(): half = add_low(shard, lax.ppermute(shard, 'narrow', [(0, 1), (3, 2)]))]
    reduce_sum x10 -> x0, other arithmetic: 9.27 us -> none  [the longest x1 3.04 us: local(): totals = jnp.sum(shifted, axis=-1, keepdims=True)]
    reshape x6 -> x1, local copies, waits for them, and re-layouts: 9.89 us -> 0.87 us  [local(): column = segments.reshape(length, 1)]
  transfers between devices with their start and end apart: 41 -> 53, of which waited for: 16 -> 19; matrix products, arithmetic and copies ran while one was open for 46% -> 5% of each run, Pallas kernels for 0% -> 20%
where the time goes in v2:
time: 292 us; the launch traced here: 291 us
  waiting for transfers between devices  115 us (39%)
  Pallas kernels  77.7 us (27%)
  starting transfers between devices  54.2 us (19%)
  local copies, waits for them, and re-layouts  31.1 us (11%)
  other arithmetic  9.13 us (3%)
  between operations  4.06 us (1%)
    pallas_call x15, Pallas kernels, call(): pl.pallas_call(kernel, out_shape=shapes, grid_spec=pltpu.PrefetchScalarGr...  77.7 us
    ppermute x38, waiting for transfers between devices, swap(): lax.ppermute(values, 'wide', [(i, i ^ bit) for i in range(lax.axis_size('...  53.3 us
    ppermute x5, waiting for transfers between devices, sum_narrow(): outer = lax.ppermute(total, 'narrow', [(1, 0), (2, 3)])  38.9 us
    ppermute x38, starting transfers between devices, swap(): lax.ppermute(values, 'wide', [(i, i ^ bit) for i in range(lax.axis_size('...  31.1 us
    unnamed x112, local copies, waits for them, and re-layouts  23.1 us
    ppermute x5, waiting for transfers between devices, sum_narrow(): half = add_low(shard, lax.ppermute(shard, 'narrow', [(0, 1), (3, 2)]))  22.4 us
    ppermute x5, starting transfers between devices, sum_narrow(): half = add_low(shard, lax.ppermute(shard, 'narrow', [(0, 1), (3, 2)]))  13.1 us
    convert_element_type x22, other arithmetic, add_low(): return sum((part.astype(F32) for part in parts)).astype(BF16)  6.82 us
  transfers between devices with their start and end apart: 53, of which 19 were waited for; matrix products, arithmetic and copies ran while one was open for 5% of the time, Pallas kernels for 20%

profile of v2, /device:TPU:0, one launch (start us, length us, event | category | flops | bytes accessed | tf_op | source)
XLA Modules:
  0.0 290.8 jit_solution(4632049924664616147)
XLA Ops:
  2.9 3.0 %collective-permute-start.9 = (bf16[80,2560]{1,0:T(8,128)(2,1)}, bf16[80,2560]{1,0:T(8,128)(2,1)S(1)}, u32[]{:S(2)}, u32[]{:S(2)}) collective-permute-start(bf16[80,2560]{1,0:T(8,128)(2,1)} %get-tuple-element.76.refs_0_), channel_id=1, source_target_pairs={{0,4},{1,5},{2,6},{3,7},{4,0},{5,1},{6,2},{7,3},{8,12},{9,13},{10,... | collective-permute-start | bytes 1228808 | tf_op jit(solution)/shard_map/ppermute | solution.py:659
  11.3 2.1 collective-permute-start.2
  13.5 2.9 %collective-permute-done.9.refs_2_ = bf16[80,2560]{1,0:T(8,128)(2,1)S(1)} collective-permute-done((bf16[80,2560]{1,0:T(8,128)(2,1)}, bf16[80,2560]{1,0:T(8,128)(2,1)S(1)}, u32[]{:S(2)}, u32[]{:S(2)}) %collective-permute-start.9) | collective-permute-done | bytes 409632 | tf_op jit(solution)/shard_map/ppermute | solution.py:659
  19.3 8.3 %collective-permute-done.refs_1_ = bf16[88,2560]{1,0:T(8,128)(2,1)S(1)} collective-permute-done((bf16[88,2560]{1,0:T(8,128)(2,1)S(1)}, bf16[88,2560]{1,0:T(8,128)(2,1)S(1)}, u32[]{:S(2)}, u32[]{:S(2)}) %collective-permute-start) | collective-permute-done | bytes 450592 | tf_op jit(solution)/shard_map/ppermute | solution.py:659
  29.6 7.1 %collective-permute-done.2.refs_3_ = bf16[88,2560]{1,0:T(8,128)(2,1)S(1)} collective-permute-done((bf16[88,2560]{1,0:T(8,128)(2,1)S(1)}, bf16[88,2560]{1,0:T(8,128)(2,1)S(1)}, u32[]{:S(2)}, u32[]{:S(2)}) %collective-permute-start.2) | collective-permute-done | bytes 450592 | tf_op jit(solution)/shard_map/ppermute | solution.py:659
  52.1 4.5 %shard_map.306 = (bf16[512,640]{1,0:T(8,128)(2,1)S(1)}, bf16[512,1920]{1,0:T(8,128)(2,1)S(1)}, bf16[640,1920]{1,0:T(8,128)(2,1)S(1)}, bf16[640,640]{1,0:T(8,128)...) custom-call(s32[8]{0:T(128)S(1)} %pad_add_fusion.position_ref, bf16[512,640]{1,0:T(8,128)(2,1)S(1)} %bitcast.56, ...), custom_call_target="tpu_custom_call" | custom-call | flops 1 | bytes 1 | tf_op jit(solution)/shard_map/pallas_call | solution.py:47
  56.7 7.9 %shard_map.307 = (bf16[512,640]{1,0:T(8,128)(2,1)S(1)}, f32[640,512]{1,0:T(8,128)S(1)}, f32[40,512]{1,0:T(8,128)S(1)}) custom-call(s32[512,1]{1,0:T(8,128)S(1)} %copy-done.13, s32[1,512]{1,0:T(1,128)S(1)} %copy-done.49, bf16[512,1920]{1,0:T(8,128)(2,1)S(1)} %get-tuple-element.69.q_ref.k_ref.v_ref, bf16[512,1920]{1,0:T(8,128)(2,1)S(1)} %get-tuple-element.69.q_ref.k_ref.v_ref, ...), custom_call_target="tpu_custom_call" | custom-call | flops 1 | bytes 1 | tf_op jit(solution)/shard_map/pallas_call | solution.py:47
  73.7 5.8 %collective-permute-done.10.refs_3_ = bf16[80,2560]{1,0:T(8,128)(2,1)S(1)} collective-permute-done((bf16[80,2560]{1,0:T(8,128)(2,1)S(1)}, bf16[80,2560]{1,0:T(8,128)(2,1)S(1)}, u32[]{:S(2)}, u32[]{:S(2)}) %collective-permute-start.10) | collective-permute-done | bytes 409632 | tf_op jit(solution)/shard_map/ppermute | solution.py:659
  80.6 8.9 %shard_map.310 = (bf16[1024,2560]{1,0:T(8,128)(2,1)S(1)}, bf16[1024,2560]{1,0:T(8,128)(2,1)S(1)}, bf16[640,2560]{1,0:T(8,128)(2,1)S(1)}) custom-call(s32[8]{0:T(128)S(1)} %pad_add_fusion.position_ref, bf16[512,640]{1,0:T(8,128)(2,1)S(1)} %get-tuple-element.74.own_ref.second_ref, bf16[512,640]{1,0:T(8,128)(2,1)S(1)} %collective-permute-done.7.other_ref.second_other_ref, ...), custom_call_target="tpu_custom_call" | custom-call | flops 1 | bytes 1 | tf_op jit(solution)/shard_map/pallas_call | solution.py:47
  89.5 8.0 %shard_map.311 = (f32[512,640]{1,0:T(8,128)S(1)}, bf16[512,640]{1,0:T(8,128)(2,1)S(1)}, bf16[2560,640]{1,0:T(8,128)(2,1)S(1)}) custom-call(s32[5]{0:T(128)S(1)} %pad_add_fusion.1.position_ref, bf16[1024,2560]{1,0:T(8,128)(2,1)S(1)} %get-tuple-element.78.act_ref, bf16[640,640]{1,0:T(8,128)(2,1)} %refs_0_.1, bf16[640,640]{1,0:T(8,128)(2,1)} %collective-permute-done.15.refs_1_, ...), custom_call_target="tpu_custom_call" | custom-call | flops 1 | bytes 1 | tf_op jit(solution)/shard_map/pallas_call | solution.py:47
  97.6 2.1 collective-permute-done.19.got_ref
  102.7 2.0 collective-permute-done.20.other_ref
  104.6 10.7 %shard_map.313 = (bf16[1024,2560]{1,0:T(8,128)(2,1)S(1)}, f32[1,2560]{1,0:T(1,128)S(1)}, bf16[2,80,2560]{2,1,0:T(8,128)(2,1)S(1)}, bf16[2,80,2560]{2,1,0:T(8,128...) custom-call(s32[1]{0:T(128)} %bitcast.13.position_ref, ...), custom_call_target="tpu_custom_call" | custom-call | flops 1 | bytes 1 | tf_op jit(solution)/shard_map/pallas_call | solution.py:47
  116.0 4.2 %shard_map.314 = (f32[512,640]{1,0:T(8,128)S(1)}, bf16[512,640]{1,0:T(8,128)(2,1)}) custom-call(bf16[1024,2560]{1,0:T(8,128)(2,1)S(1)} %get-tuple-element.86.grad_ref, bf16[640,2560]{1,0:T(8,128)(2,1)S(1)} %get-tuple-element.87.up_ref), custom_call_target="tpu_custom_call" | custom-call | flops 1 | bytes 1 | tf_op jit(solution)/shard_map/pallas_call | solution.py:47
  122.0 2.5 copy-done.1
  126.6 4.3 %shard_map.319 = (bf16[2,320,640]{2,1,0:T(8,128)(2,1)S(1)}, bf16[2,320,640]{2,1,0:T(8,128)(2,1)S(1)}, bf16[2,320,640]{2,1,0:T(8,128)(2,1)S(1)}, bf16[2,320,640]{2,1,0:T(8,128)(2,1)S(1)}) custom-call(s32[1]{0:T(128)} %bitcast.13.position_ref, bf16[1024,2560]{1,0:T(8,128)(2,1)S(1)} %copy-done.1, bf16[512,640]{1,0:T(8,128)(2,1)S(1)} %copy-done.8, ...), custom_call_target="tpu_custom_call" | custom-call | flops 1 | bytes 1 | tf_op jit(solution)/shard_map/pallas_call | solution.py:47
  134.0 3.0 %shard_map.315 = (f32[512,640]{1,0:T(8,128)S(1)}, bf16[512,640]{1,0:T(8,128)(2,1)S(1)}, bf16[512,640]{1,0:T(8,128)(2,1)S(1)}, f32[8,640]{1,0:T(8,128)S(1)}) custom-call(f32[512,640]{1,0:T(8,128)S(1)} %copy-done.22, bf16[512,640]{1,0:T(8,128)(2,1)} %collective-permute-done.21.got_ref, f32[512,640]{1,0:T(8,128)S(1)} %copy-done.4, f32[512,640]{1,0:T(8,128)S(1)} %copy-done.20, ...), custom_call_target="tpu_custom_call" | custom-call | flops 1 | bytes 1 | tf_op jit(solution)/shard_map/pallas_call | solution.py:47
  137.1 13.3 %shard_map.316 = (bf16[512,640]{1,0:T(8,128)(2,1)S(1)}, bf16[512,640]{1,0:T(8,128)(2,1)S(1)}, bf16[512,640]{1,0:T(8,128)(2,1)S(1)}) custom-call(s32[512,1]{1,0:T(8,128)S(1)} %copy-done.14, s32[1,512]{1,0:T(1,128)S(1)} %copy-done.49, bf16[512,1920]{1,0:T(8,128)(2,1)S(1)} %get-tuple-element.69.q_ref.k_ref.v_ref, ...), custom_call_target="tpu_custom_call" | custom-call | flops 1 | bytes 1 | tf_op jit(solution)/shard_map/pallas_call | solution.py:47
  150.4 8.3 %shard_map.317 = (bf16[88,2560]{1,0:T(8,128)(2,1)S(1)}, bf16[88,2560]{1,0:T(8,128)(2,1)S(1)}, bf16[88,2560]{1,0:T(8,128)(2,1)S(1)}, bf16[88,2560]{1,0:T(8,128)(2...) custom-call(s32[8]{0:T(128)S(1)} %pad_add_fusion.position_ref, ...), custom_call_target="tpu_custom_call" | custom-call | flops 1 | bytes 1 | tf_op jit(solution)/shard_map/pallas_call | solution.py:47
  167.1 15.9 %collective-permute-done.38 = bf16[80,2560]{1,0:T(8,128)(2,1)S(1)} collective-permute-done((bf16[80,2560]{1,0:T(8,128)(2,1)S(1)}, bf16[80,2560]{1,0:T(8,128)(2,1)S(1)}, u32[]{:S(2)}, u32[]{:S(2)}) %collective-permute-start.38) | collective-permute-done | bytes 409632 | tf_op jit(solution)/shard_map/ppermute | solution.py:659
  183.0 2.0 collective-permute-start.24
  189.1 3.5 %collective-permute-start.45 = (bf16[320,640]{1,0:T(8,128)(2,1)S(1)}, bf16[320,640]{1,0:T(8,128)(2,1)S(1)}, u32[]{:S(2)}, u32[]{:S(2)}) collective-permute-start(bf16[320,640]{1,0:T(8,128)(2,1)S(1)} %fusion.1), channel_id=1, source_target_pairs={{0,8},{24,16},{1,9},{25,17},{2,10},{26,18},{3,11},{27,19},{4,12},{... | collective-permute-start | bytes 1228808 | tf_op jit(solution)/shard_map/ppermute | solution.py:698
  194.1 3.0 %collective-permute-done.24 = bf16[88,2560]{1,0:T(8,128)(2,1)S(1)} collective-permute-done((bf16[88,2560]{1,0:T(8,128)(2,1)S(1)}, bf16[88,2560]{1,0:T(8,128)(2,1)S(1)}, u32[]{:S(2)}, u32[]{:S(2)}) %collective-permute-start.24) | collective-permute-done | bytes 450592 | tf_op jit(solution)/shard_map/ppermute | solution.py:659
  197.1 3.5 %collective-permute-start.39 = (bf16[80,2560]{1,0:T(8,128)(2,1)S(1)}, bf16[80,2560]{1,0:T(8,128)(2,1)S(1)}, u32[]{:S(2)}, u32[]{:S(2)}) collective-permute-start(bf16[80,2560]{1,0:T(8,128)(2,1)S(1)} %fusion.2), channel_id=1, source_target_pairs={{0,8},{24,16},{1,9},{25,17},{2,10},{26,18},{3,11},{27,19},{4,12},{... | collective-permute-start | bytes 1228808 | tf_op jit(solution)/shard_map/ppermute | solution.py:698
  200.6 4.2 %collective-permute-done.26 = bf16[88,2560]{1,0:T(8,128)(2,1)S(1)} collective-permute-done((bf16[88,2560]{1,0:T(8,128)(2,1)S(1)}, bf16[88,2560]{1,0:T(8,128)(2,1)S(1)}, u32[]{:S(2)}, u32[]{:S(2)}) %collective-permute-start.26) | collective-permute-done | bytes 450592 | tf_op jit(solution)/shard_map/ppermute | solution.py:659
  204.8 3.5 %collective-permute-start.34 = (bf16[80,2560]{1,0:T(8,128)(2,1)S(1)}, bf16[80,2560]{1,0:T(8,128)(2,1)S(1)}, u32[]{:S(2)}, u32[]{:S(2)}) collective-permute-start(bf16[80,2560]{1,0:T(8,128)(2,1)S(1)} %fusion.3), channel_id=1, source_target_pairs={{0,8},{24,16},{1,9},{25,17},{2,10},{26,18},{3,11},{27,19},{4,12},{... | collective-permute-start | bytes 1228808 | tf_op jit(solution)/shard_map/ppermute | solution.py:698
  212.0 8.0 %collective-permute-done.39 = bf16[80,2560]{1,0:T(8,128)(2,1)S(1)} collective-permute-done((bf16[80,2560]{1,0:T(8,128)(2,1)S(1)}, bf16[80,2560]{1,0:T(8,128)(2,1)S(1)}, u32[]{:S(2)}, u32[]{:S(2)}) %collective-permute-start.39) | collective-permute-done | bytes 409632 | tf_op jit(solution)/shard_map/ppermute | solution.py:698
  220.8 8.0 %collective-permute-done.34 = bf16[80,2560]{1,0:T(8,128)(2,1)S(1)} collective-permute-done((bf16[80,2560]{1,0:T(8,128)(2,1)S(1)}, bf16[80,2560]{1,0:T(8,128)(2,1)S(1)}, u32[]{:S(2)}, u32[]{:S(2)}) %collective-permute-start.34) | collective-permute-done | bytes 409632 | tf_op jit(solution)/shard_map/ppermute | solution.py:698
  229.6 6.0 %collective-permute-done.29 = bf16[88,2560]{1,0:T(8,128)(2,1)S(1)} collective-permute-done((bf16[88,2560]{1,0:T(8,128)(2,1)S(1)}, bf16[88,2560]{1,0:T(8,128)(2,1)S(1)}, u32[]{:S(2)}, u32[]{:S(2)}) %collective-permute-start.29) | collective-permute-done | bytes 450592 | tf_op jit(solution)/shard_map/ppermute | solution.py:698
  243.5 27.4 %collective-permute-done.41 = bf16[80,2560]{1,0:T(8,128)(2,1)S(1)} collective-permute-done((bf16[80,2560]{1,0:T(8,128)(2,1)S(1)}, bf16[80,2560]{1,0:T(8,128)(2,1)S(1)}, u32[]{:S(2)}, u32[]{:S(2)}) %collective-permute-start.41) | collective-permute-done | bytes 409632 | tf_op jit(solution)/shard_map/ppermute | solution.py:700
  270.9 8.8 %collective-permute-done.36 = bf16[80,2560]{1,0:T(8,128)(2,1)S(1)} collective-permute-done((bf16[80,2560]{1,0:T(8,128)(2,1)S(1)}, bf16[80,2560]{1,0:T(8,128)(2,1)S(1)}, u32[]{:S(2)}, u32[]{:S(2)}) %collective-permute-start.36) | collective-permute-done | bytes 409632 | tf_op jit(solution)/shard_map/ppermute | solution.py:700
  282.9 2.7 collective-permute-done.31
  (242 shorter events, 81.4 us)
Async XLA Ops:
  11.3 25.4 %collective-permute-start.2 = (bf16[88,2560]{1,0:T(8,128)(2,1)S(1)}, bf16[88,2560]{1,0:T(8,128)(2,1)S(1)}, u32[]{:S(2)}, u32[]{:S(2)}) collective-permute-start(bf16[88,2560]{1,0:T(8,128)(2,1)S(1)} %shard_map.305.refs_0_), channel_id=1, source_target_pairs={{0,6},{1,7},{2,4},{3,5},{4,2},{5,3},{6,0},{7,1},{8,14},{9,15},{10,... | collective-permute-start | bytes 1351688 | tf_op jit(solution)/shard_map/ppermute | solution.py:659
  16.4 21.1 %collective-permute-start.3 = (bf16[88,2560]{1,0:T(8,128)(2,1)S(1)}, bf16[88,2560]{1,0:T(8,128)(2,1)S(1)}, u32[]{:S(2)}, u32[]{:S(2)}) collective-permute-start(bf16[88,2560]{1,0:T(8,128)(2,1)S(1)} %shard_map.305.refs_0_), channel_id=1, source_target_pairs={{0,1},{1,0},{2,3},{3,2},{4,5},{5,4},{6,7},{7,6},{8,9},{9,8},{10,11... | collective-permute-start | bytes 1351688 | tf_op jit(solution)/shard_map/ppermute | solution.py:659
  17.8 47.9 %collective-permute-start.16 = (bf16[640,640]{1,0:T(8,128)(2,1)}, bf16[640,640]{1,0:T(8,128)(2,1)}, u32[]{:S(2)}, u32[]{:S(2)}) collective-permute-start(bf16[640,640]{1,0:T(8,128)(2,1)} %refs_0_.1), channel_id=1, source_target_pairs={{0,4},{1,5},{2,6},{3,7},{4,0},{5,1},{6,2},{7,3},{8,12},{9,13},{10,... | collective-permute-start | bytes 2457608 | tf_op jit(solution)/shard_map/ppermute | solution.py:659
  38.3 30.0 %collective-permute-start.15 = (bf16[640,640]{1,0:T(8,128)(2,1)}, bf16[640,640]{1,0:T(8,128)(2,1)}, u32[]{:S(2)}, u32[]{:S(2)}) collective-permute-start(bf16[640,640]{1,0:T(8,128)(2,1)} %refs_0_.1), channel_id=1, source_target_pairs={{0,2},{1,3},{2,0},{3,1},{4,6},{5,7},{6,4},{7,5},{8,10},{9,11},{10,... | collective-permute-start | bytes 2457608 | tf_op jit(solution)/shard_map/ppermute | solution.py:659
  40.6 26.5 %collective-permute-start.11 = (bf16[80,2560]{1,0:T(8,128)(2,1)}, bf16[80,2560]{1,0:T(8,128)(2,1)}, u32[]{:S(2)}, u32[]{:S(2)}) collective-permute-start(bf16[80,2560]{1,0:T(8,128)(2,1)} %get-tuple-element.77), channel_id=1, source_target_pairs={{0,1},{1,0},{2,3},{3,2},{4,5},{5,4},{6,7},{7,6},{8,9},{9,8},{10,11... | collective-permute-start | bytes 1228808 | tf_op jit(solution)/shard_map/ppermute | solution.py:659
  41.5 28.3 %collective-permute-start.13 = (bf16[80,2560]{1,0:T(8,128)(2,1)}, bf16[80,2560]{1,0:T(8,128)(2,1)}, u32[]{:S(2)}, u32[]{:S(2)}) collective-permute-start(bf16[80,2560]{1,0:T(8,128)(2,1)} %get-tuple-element.77), channel_id=1, source_target_pairs={{0,5},{1,4},{2,7},{3,6},{4,1},{5,0},{6,3},{7,2},{8,13},{9,12},{10,... | collective-permute-start | bytes 1228808 | tf_op jit(solution)/shard_map/ppermute | solution.py:659
  43.0 27.5 %collective-permute-start.8 = (bf16[80,2560]{1,0:T(8,128)(2,1)}, bf16[80,2560]{1,0:T(8,128)(2,1)}, u32[]{:S(2)}, u32[]{:S(2)}) collective-permute-start(bf16[80,2560]{1,0:T(8,128)(2,1)} %get-tuple-element.76.refs_0_), channel_id=1, source_target_pairs={{0,2},{1,3},{2,0},{3,1},{4,6},{5,7},{6,4},{7,5},{8,10},{9,11},{10,... | collective-permute-start | bytes 1228808 | tf_op jit(solution)/shard_map/ppermute | solution.py:659
  69.8 19.7 %collective-permute-start.17 = (bf16[320,640]{1,0:T(8,128)(2,1)S(1)}, bf16[320,640]{1,0:T(8,128)(2,1)S(1)}, u32[]{:S(2)}, u32[]{:S(2)}) collective-permute-start(bf16[320,640]{1,0:T(8,128)(2,1)S(1)} %slice.145), channel_id=1, source_target_pairs={{0,2},{1,3},{2,0},{3,1},{4,6},{5,7},{6,4},{7,5},{8,10},{9,11},{10,... | collective-permute-start | bytes 1228808 | tf_op jit(solution)/shard_map/ppermute | solution.py:659
  70.5 19.0 %collective-permute-start.18 = (bf16[320,640]{1,0:T(8,128)(2,1)S(1)}, bf16[320,640]{1,0:T(8,128)(2,1)S(1)}, u32[]{:S(2)}, u32[]{:S(2)}) collective-permute-start(bf16[320,640]{1,0:T(8,128)(2,1)S(1)} %slice.146), channel_id=1, source_target_pairs={{0,4},{1,5},{2,6},{3,7},{4,0},{5,1},{6,2},{7,3},{8,12},{9,13},{10,... | collective-permute-start | bytes 1228808 | tf_op jit(solution)/shard_map/ppermute | solution.py:659
  115.4 43.3 %collective-permute-start.37 = (bf16[2,80,2560]{2,1,0:T(8,128)(2,1)}, bf16[2,80,2560]{2,1,0:T(8,128)(2,1)}, u32[]{:S(2)}, u32[]{:S(2)}) collective-permute-start(bf16[2,80,2560]{2,1,0:T(8,128)(2,1)} %get-tuple-element.116), channel_id=1, source_target_pairs={{0,4},{1,5},{2,6},{3,7},{4,0},{5,1},{6,2},{7,3},{8,12},{9,13},{10,... | collective-permute-start | bytes 2457608 | tf_op jit(solution)/shard_map/ppermute | solution.py:659
  121.3 39.1 %collective-permute-start.32 = (bf16[2,80,2560]{2,1,0:T(8,128)(2,1)}, bf16[2,80,2560]{2,1,0:T(8,128)(2,1)}, u32[]{:S(2)}, u32[]{:S(2)}) collective-permute-start(bf16[2,80,2560]{2,1,0:T(8,128)(2,1)} %get-tuple-element.114), channel_id=1, source_target_pairs={{0,2},{1,3},{2,0},{3,1},{4,6},{5,7},{6,4},{7,5},{8,10},{9,11},{10,... | collective-permute-start | bytes 2457608 | tf_op jit(solution)/shard_map/ppermute | solution.py:659
  130.9 30.7 %collective-permute-start.43 = (bf16[2,320,640]{2,1,0:T(8,128)(2,1)S(1)}, bf16[2,320,640]{2,1,0:T(8,128)(2,1)S(1)}, u32[]{:S(2)}, u32[]{:S(2)}) collective-permute-start(bf16[2,320,640]{2,1,0:T(8,128)(2,1)S(1)} %get-tuple-element.118), channel_id=1, source_target_pairs={{0,2},{1,3},{2,0},{3,1},{4,6},{5,7},{6,4},{7,5},{8,10},{9,11},{10,... | collective-permute-start | bytes 2457608 | tf_op jit(solution)/shard_map/ppermute | solution.py:659
  132.4 29.9 %collective-permute-start.48 = (bf16[2,320,640]{2,1,0:T(8,128)(2,1)S(1)}, bf16[2,320,640]{2,1,0:T(8,128)(2,1)S(1)}, u32[]{:S(2)}, u32[]{:S(2)}) collective-permute-start(bf16[2,320,640]{2,1,0:T(8,128)(2,1)S(1)} %get-tuple-element.120), channel_id=1, source_target_pairs={{0,4},{1,5},{2,6},{3,7},{4,0},{5,1},{6,2},{7,3},{8,12},{9,13},{10,... | collective-permute-start | bytes 2457608 | tf_op jit(solution)/shard_map/ppermute | solution.py:659
  161.6 31.2 %collective-permute-start.22 = (bf16[88,2560]{1,0:T(8,128)(2,1)S(1)}, bf16[88,2560]{1,0:T(8,128)(2,1)S(1)}, u32[]{:S(2)}, u32[]{:S(2)}) collective-permute-start(bf16[88,2560]{1,0:T(8,128)(2,1)S(1)} %get-tuple-element.106), channel_id=1, source_target_pairs={{0,1},{1,0},{2,3},{3,2},{4,5},{5,4},{6,7},{7,6},{8,9},{9,8},{10,11... | collective-permute-start | bytes 1351688 | tf_op jit(solution)/shard_map/ppermute | solution.py:659
  162.3 26.1 %collective-permute-start.44 = (bf16[320,640]{1,0:T(8,128)(2,1)S(1)}, bf16[320,640]{1,0:T(8,128)(2,1)S(1)}, u32[]{:S(2)}, u32[]{:S(2)}) collective-permute-start(bf16[320,640]{1,0:T(8,128)(2,1)S(1)} %fusion.6), channel_id=1, source_target_pairs={{0,4},{1,5},{2,6},{3,7},{4,0},{5,1},{6,2},{7,3},{8,12},{9,13},{10,... | collective-permute-start | bytes 1228808 | tf_op jit(solution)/shard_map/ppermute | solution.py:659
  163.0 26.1 %collective-permute-start.49 = (bf16[320,640]{1,0:T(8,128)(2,1)S(1)}, bf16[320,640]{1,0:T(8,128)(2,1)S(1)}, u32[]{:S(2)}, u32[]{:S(2)}) collective-permute-start(bf16[320,640]{1,0:T(8,128)(2,1)S(1)} %fusion.7), channel_id=1, source_target_pairs={{0,2},{1,3},{2,0},{3,1},{4,6},{5,7},{6,4},{7,5},{8,10},{9,11},{10,... | collective-permute-start | bytes 1228808 | tf_op jit(solution)/shard_map/ppermute | solution.py:659
  163.8 19.2 %collective-permute-start.38 = (bf16[80,2560]{1,0:T(8,128)(2,1)S(1)}, bf16[80,2560]{1,0:T(8,128)(2,1)S(1)}, u32[]{:S(2)}, u32[]{:S(2)}) collective-permute-start(bf16[80,2560]{1,0:T(8,128)(2,1)S(1)} %fusion.5), channel_id=1, source_target_pairs={{0,2},{1,3},{2,0},{3,1},{4,6},{5,7},{6,4},{7,5},{8,10},{9,11},{10,... | collective-permute-start | bytes 1228808 | tf_op jit(solution)/shard_map/ppermute | solution.py:659
  165.4 20.7 %collective-permute-start.33 = (bf16[80,2560]{1,0:T(8,128)(2,1)S(1)}, bf16[80,2560]{1,0:T(8,128)(2,1)S(1)}, u32[]{:S(2)}, u32[]{:S(2)}) collective-permute-start(bf16[80,2560]{1,0:T(8,128)(2,1)S(1)} %fusion.4), channel_id=1, source_target_pairs={{0,4},{1,5},{2,6},{3,7},{4,0},{5,1},{6,2},{7,3},{8,12},{9,13},{10,... | collective-permute-start | bytes 1228808 | tf_op jit(solution)/shard_map/ppermute | solution.py:659
  186.1 18.7 %collective-permute-start.26 = (bf16[88,2560]{1,0:T(8,128)(2,1)S(1)}, bf16[88,2560]{1,0:T(8,128)(2,1)S(1)}, u32[]{:S(2)}, u32[]{:S(2)}) collective-permute-start(bf16[88,2560]{1,0:T(8,128)(2,1)S(1)} %add_convert_fusion.4), channel_id=1, source_target_pairs={{0,2},{1,3},{2,0},{3,1},{4,6},{5,7},{6,4},{7,5},{8,10},{9,11},{10,... | collective-permute-start | bytes 1351688 | tf_op jit(solution)/shard_map/ppermute | solution.py:659
  188.4 19.9 %collective-permute-start.28 = (bf16[88,2560]{1,0:T(8,128)(2,1)S(1)}, bf16[88,2560]{1,0:T(8,128)(2,1)S(1)}, u32[]{:S(2)}, u32[]{:S(2)}) collective-permute-start(bf16[88,2560]{1,0:T(8,128)(2,1)S(1)} %add_convert_fusion.3), channel_id=1, source_target_pairs={{0,4},{1,5},{2,6},{3,7},{4,0},{5,1},{6,2},{7,3},{8,12},{9,13},{10,... | collective-permute-start | bytes 1351688 | tf_op jit(solution)/shard_map/ppermute | solution.py:659
  189.1 20.9 %collective-permute-start.45 = (bf16[320,640]{1,0:T(8,128)(2,1)S(1)}, bf16[320,640]{1,0:T(8,128)(2,1)S(1)}, u32[]{:S(2)}, u32[]{:S(2)}) collective-permute-start(bf16[320,640]{1,0:T(8,128)(2,1)S(1)} %fusion.1), channel_id=1, source_target_pairs={{0,8},{24,16},{1,9},{25,17},{2,10},{26,18},{3,11},{27,19},{4,12},{... | collective-permute-start | bytes 1228808 | tf_op jit(solution)/shard_map/ppermute | solution.py:698
  197.1 22.9 %collective-permute-start.39 = (bf16[80,2560]{1,0:T(8,128)(2,1)S(1)}, bf16[80,2560]{1,0:T(8,128)(2,1)S(1)}, u32[]{:S(2)}, u32[]{:S(2)}) collective-permute-start(bf16[80,2560]{1,0:T(8,128)(2,1)S(1)} %fusion.2), channel_id=1, source_target_pairs={{0,8},{24,16},{1,9},{25,17},{2,10},{26,18},{3,11},{27,19},{4,12},{... | collective-permute-start | bytes 1228808 | tf_op jit(solution)/shard_map/ppermute | solution.py:698
  204.8 24.0 %collective-permute-start.34 = (bf16[80,2560]{1,0:T(8,128)(2,1)S(1)}, bf16[80,2560]{1,0:T(8,128)(2,1)S(1)}, u32[]{:S(2)}, u32[]{:S(2)}) collective-permute-start(bf16[80,2560]{1,0:T(8,128)(2,1)S(1)} %fusion.3), channel_id=1, source_target_pairs={{0,8},{24,16},{1,9},{25,17},{2,10},{26,18},{3,11},{27,19},{4,12},{... | collective-permute-start | bytes 1228808 | tf_op jit(solution)/shard_map/ppermute | solution.py:698
  208.7 26.9 %collective-permute-start.29 = (bf16[88,2560]{1,0:T(8,128)(2,1)S(1)}, bf16[88,2560]{1,0:T(8,128)(2,1)S(1)}, u32[]{:S(2)}, u32[]{:S(2)}) collective-permute-start(bf16[88,2560]{1,0:T(8,128)(2,1)S(1)} %add_convert_fusion.2), channel_id=1, source_target_pairs={{0,8},{24,16},{1,9},{25,17},{2,10},{26,18},{3,11},{27,19},{4,12},{... | collective-permute-start | bytes 1351688 | tf_op jit(solution)/shard_map/ppermute | solution.py:698
  210.1 26.3 %collective-permute-start.46 = (bf16[320,640]{1,0:T(8,128)(2,1)S(1)}, bf16[320,640]{1,0:T(8,128)(2,1)S(1)}, u32[]{:S(2)}, u32[]{:S(2)}) collective-permute-start(bf16[320,640]{1,0:T(8,128)(2,1)S(1)} %add_convert_fusion.11), channel_id=1, source_target_pairs={{8,16},{16,8},{9,17},{17,9},{10,18},{18,10},{11,19},{19,11},{12,20... | collective-permute-start | bytes 1228808 | tf_op jit(solution)/shard_map/ppermute | solution.py:699
  211.3 26.5 %collective-permute-start.51 = (bf16[320,640]{1,0:T(8,128)(2,1)S(1)}, bf16[320,640]{1,0:T(8,128)(2,1)S(1)}, u32[]{:S(2)}, u32[]{:S(2)}) collective-permute-start(bf16[320,640]{1,0:T(8,128)(2,1)S(1)} %add_convert_fusion.8), channel_id=1, source_target_pairs={{8,16},{16,8},{9,17},{17,9},{10,18},{18,10},{11,19},{19,11},{12,20... | collective-permute-start | bytes 1228808 | tf_op jit(solution)/shard_map/ppermute | solution.py:699
  220.1 19.1 %collective-permute-start.40 = (bf16[80,2560]{1,0:T(8,128)(2,1)S(1)}, bf16[80,2560]{1,0:T(8,128)(2,1)S(1)}, u32[]{:S(2)}, u32[]{:S(2)}) collective-permute-start(bf16[80,2560]{1,0:T(8,128)(2,1)S(1)} %add_convert_fusion.14), channel_id=1, source_target_pairs={{8,16},{16,8},{9,17},{17,9},{10,18},{18,10},{11,19},{19,11},{12,20... | collective-permute-start | bytes 1228808 | tf_op jit(solution)/shard_map/ppermute | solution.py:699
  236.5 43.4 %collective-permute-start.47 = (bf16[320,640]{1,0:T(8,128)(2,1)S(1)}, bf16[320,640]{1,0:T(8,128)(2,1)S(1)}, u32[]{:S(2)}, u32[]{:S(2)}) collective-permute-start(bf16[320,640]{1,0:T(8,128)(2,1)S(1)} %add_convert_fusion.10), channel_id=1, source_target_pairs={{8,0},{16,24},{9,1},{17,25},{10,2},{18,26},{11,3},{19,27},{12,4},{... | collective-permute-start | bytes 1228808 | tf_op jit(solution)/shard_map/ppermute | solution.py:700
  237.9 42.0 %collective-permute-start.52 = (bf16[320,640]{1,0:T(8,128)(2,1)S(1)}, bf16[320,640]{1,0:T(8,128)(2,1)S(1)}, u32[]{:S(2)}, u32[]{:S(2)}) collective-permute-start(bf16[320,640]{1,0:T(8,128)(2,1)S(1)} %add_convert_fusion.7), channel_id=1, source_target_pairs={{8,0},{16,24},{9,1},{17,25},{10,2},{18,26},{11,3},{19,27},{12,4},{... | collective-permute-start | bytes 1228808 | tf_op jit(solution)/shard_map/ppermute | solution.py:700
  239.3 31.6 %collective-permute-start.41 = (bf16[80,2560]{1,0:T(8,128)(2,1)S(1)}, bf16[80,2560]{1,0:T(8,128)(2,1)S(1)}, u32[]{:S(2)}, u32[]{:S(2)}) collective-permute-start(bf16[80,2560]{1,0:T(8,128)(2,1)S(1)} %add_convert_fusion.13), channel_id=1, source_target_pairs={{8,0},{16,24},{9,1},{17,25},{10,2},{18,26},{11,3},{19,27},{12,4},{... | collective-permute-start | bytes 1228808 | tf_op jit(solution)/shard_map/ppermute | solution.py:700
  240.8 39.0 %collective-permute-start.36 = (bf16[80,2560]{1,0:T(8,128)(2,1)S(1)}, bf16[80,2560]{1,0:T(8,128)(2,1)S(1)}, u32[]{:S(2)}, u32[]{:S(2)}) collective-permute-start(bf16[80,2560]{1,0:T(8,128)(2,1)S(1)} %add_convert_fusion.16), channel_id=1, source_target_pairs={{8,0},{16,24},{9,1},{17,25},{10,2},{18,26},{11,3},{19,27},{12,4},{... | collective-permute-start | bytes 1228808 | tf_op jit(solution)/shard_map/ppermute | solution.py:700
  242.2 43.4 %collective-permute-start.31 = (bf16[88,2560]{1,0:T(8,128)(2,1)S(1)}, bf16[88,2560]{1,0:T(8,128)(2,1)S(1)}, u32[]{:S(2)}, u32[]{:S(2)}) collective-permute-start(bf16[88,2560]{1,0:T(8,128)(2,1)S(1)} %add_convert_fusion), channel_id=1, source_target_pairs={{8,0},{16,24},{9,1},{17,25},{10,2},{18,26},{11,3},{19,27},{12,4},{... | collective-permute-start | bytes 1351688 | tf_op jit(solution)/shard_map/ppermute | solution.py:700
  (77 other events, 589.8 us)
